TPU v7x, 1024 devices: a whole 4x8x16 slice. The times are simulated.
1024 devices in a mesh: batch: 32 (over z, core), col: 4 (over x), rep: 8 (over y).
Axes of the slice: x: 4, y: 8, z: 16, core: 2. Of those that a mesh axis runs over, the one named last changes fastest.
Arguments:
- lookups: bfloat16 [262144, 1024], P(('rep', 'batch'), 'col'), parts along dimension 0, may hold values from -6 to 6
- input_weight: bfloat16 [1024, 1024], replicated, may hold values from -0.1875 to 0.1875
- joined_weight: bfloat16 [1024, 2048], replicated, may hold values from -0.1875 to 0.1875
- output_weight: bfloat16 [512, 1024], replicated, may hold values from -0.25 to 0.25
- owner_counts: int32 [1024, 32], P(('rep', 'batch', 'col')), parts along dimension 0, may hold values from 1 to 12, 256 in all within a row
- user_index: int32 [262144], P(('rep', 'batch', 'col')), parts along dimension 0, may hold values from 0 to 7
Outputs:
- layer_out: bfloat16 [262144, 1024], P(('rep', 'batch', 'col')), parts along dimension 0
There are 8 independent parts, one for each index of `rep`. A program takes and returns all parts, laid end to end along the dimension named above; an argument that names none is the same for every part. Nothing has to cross between parts.
Inputs may be any that keep to these rules, and one draw needn't show every extreme that they name: `owner_counts`: each row sums to 256; every entry is 1 or more and each row reaches 12.
All inputs are finite; a program needn't handle non-finite values.
Results may differ from a plain program's by a relative error of at most 0.0071.
Values may be sent and summed in bfloat16 or wider, within the bound.
A program may use at most 32 MiB of HBM per device.

v0:
```python
import jax
import jax.numpy as jnp
from jax import lax
from jax.sharding import PartitionSpec as P

HEADS = 4
HEAD_DIM = 128


eps_norm = 1e-06


def layer_norm(values):
    row_mean = jnp.mean(values, axis=-1, keepdims=True)
    centered = values - row_mean
    row_var = jnp.mean(centered * centered, axis=-1, keepdims=True)
    return centered * lax.rsqrt(row_var + eps_norm)


def project(hidden_rows, joined_weight):
    normed = layer_norm(hidden_rows.astype(jnp.float32)).astype(jnp.bfloat16)
    return jax.nn.silu(jnp.dot(normed, joined_weight, preferred_element_type=jnp.float32)).astype(
        jnp.bfloat16
    )


def attend(joined_rows, seg_ids):
    width = HEADS * HEAD_DIM
    total = joined_rows.shape[0]
    gate_part = joined_rows[:, :width]
    value_part = joined_rows[:, width : 2 * width].reshape(total, HEADS, HEAD_DIM)
    query_part = joined_rows[:, 2 * width : 3 * width].reshape(total, HEADS, HEAD_DIM)
    key_part = joined_rows[:, 3 * width :].reshape(total, HEADS, HEAD_DIM)
    scores = jnp.einsum(
        "ihd,jhd->hij", query_part, key_part, preferred_element_type=jnp.float32
    ) * HEAD_DIM ** (-0.5)
    positions = jnp.arange(total, dtype=jnp.int32)
    allowed = (positions[None, :] <= positions[:, None]) & (seg_ids[None, :] == seg_ids[:, None])
    weights = jnp.where(allowed[None], jax.nn.silu(scores), 0.0).astype(jnp.bfloat16)
    mixed = jnp.einsum(
        "hij,jhd->ihd", weights, value_part, preferred_element_type=jnp.float32
    ).reshape(total, width)
    return (layer_norm(mixed) * gate_part.astype(jnp.float32)).astype(jnp.bfloat16)


def on_device(lookups, input_weight, joined_weight, output_weight, owner_counts, user_index):
    token_block = lax.all_to_all(lookups, "col", split_axis=0, concat_axis=1, tiled=True)
    hidden = jnp.dot(token_block, input_weight, preferred_element_type=jnp.float32).astype(
        jnp.bfloat16
    )
    local_rows = hidden.shape[0]
    owners = lax.axis_size("batch")
    capacity = local_rows // owners + local_rows // (2 * owners)
    counts = owner_counts[0]
    bin_ends = jnp.cumsum(counts)
    bin_starts = bin_ends - counts
    slot_ids = jnp.arange(capacity, dtype=jnp.int32)
    filled = slot_ids[None, :] < counts[:, None]
    gather_rows = jnp.where(filled, bin_starts[:, None] + slot_ids[None, :], 0).reshape(-1)
    seg_send = jnp.where(filled.reshape(-1), user_index[gather_rows], -1).reshape(owners, capacity)
    payload = hidden[gather_rows].reshape(owners, capacity, -1)
    received, seg_ids = (
        lax.all_to_all(payload, "batch", split_axis=0, concat_axis=0, tiled=True),
        lax.all_to_all(seg_send, "batch", split_axis=0, concat_axis=0, tiled=True),
    )
    joined_rows = project(received.reshape(owners * capacity, -1), joined_weight)
    gated_rows = attend(joined_rows, seg_ids.reshape(-1))
    token_pos = jnp.arange(local_rows, dtype=jnp.int32)
    owner_ids = jnp.arange(owners, dtype=jnp.int32)
    dest_owner = jnp.sum((token_pos[:, None] >= bin_ends[None, :]).astype(jnp.int32), axis=1)
    onehot = dest_owner[:, None] == owner_ids[None, :]
    first_slot = jnp.sum(jnp.where(onehot, bin_starts[None, :], 0), axis=1)
    back_rows = dest_owner * capacity + token_pos - first_slot
    branch = jnp.dot(gated_rows, output_weight, preferred_element_type=jnp.float32).astype(
        jnp.bfloat16
    )
    returned = lax.all_to_all(
        branch.reshape(owners, capacity, -1), "batch", split_axis=0, concat_axis=0, tiled=True
    )
    branch_rows = returned.reshape(owners * capacity, -1)[back_rows]
    return (hidden.astype(jnp.float32) + branch_rows.astype(jnp.float32)).astype(jnp.bfloat16)


def solution(mesh):
    return jax.shard_map(
        on_device,
        mesh=mesh,
        in_specs=(
            P(("rep", "batch"), "col"),
            P(),
            P(),
            P(),
            P(("rep", "batch", "col"), None),
            P(("rep", "batch", "col")),
        ),
        out_specs=P(("rep", "batch", "col"), None),
        check_vma=False,
    )
```

profile of v0, /device:TPU:1, one launch (start us, length us, event | category | flops | bytes accessed | tf_op | source)
XLA Modules:
  0.0 196.4 jit_solution(17894700376194369830)
XLA Ops:
  0.0 5.0 %all-to-all-start = ((bf16[4,256,256]{2,1,0:T(8,128)(2,1)}), bf16[4,256,256]{2,1,0:T(8,128)(2,1)S(1)}, u32[]{:S(2)}, u32[]{:S(2)}) async-start(bf16[4,256,256]{2,1,0:T(8,128)(2,1)} %bitcast.49), calls=%async_computation | async-start | bytes 1048576 | tf_op jit(solution)/shard_map/all_to_all | solution.py:47
  7.4 2.8 %gather_fusion.1 = s32[384]{0:T(512)S(1)} fusion(s32[256]{0:T(256)S(1)} %copy-done.1, s32[1024]{0:T(1024)S(1)} %pad_clamp_fusion.1), kind=kCustom, calls=%fused_computation.1 | custom fusion | bytes 4608 | tf_op jit(solution)/shard_map/gather | solution.py:60
  11.9 22.4 %all-to-all-start.2 = ((s32[32,1,12]{2,1,0:T(1,128)}), s32[32,1,12]{2,1,0:T(1,128)S(1)}, u32[]{:S(2)}, u32[]{:S(2)}) async-start(s32[32,1,12]{2,1,0:T(1,128)} %bitcast.6), calls=%async_computation.2 | async-start | bytes 32768 | tf_op jit(solution)/shard_map/all_to_all | solution.py:64
  35.3 1.8 convolution_convert_fusion.1
  37.1 2.1 %gather_fusion = bf16[384,1024]{1,0:T(8,128)(2,1)S(1)} fusion(bf16[256,1024]{1,0:T(8,128)(2,1)S(1)} %convolution_convert_fusion.1, s32[1024]{0:T(1024)S(1)} %pad_clamp_fusion.1), kind=kCustom, calls=%fused_computation | custom fusion | bytes 1574400 | tf_op jit(solution)/shard_map/gather | solution.py:61
  39.2 1.2 reshape.288
  40.4 5.7 %all-to-all-done.2 = s32[32,1,12]{2,1,0:T(1,128)S(1)} async-done(((s32[32,1,12]{2,1,0:T(1,128)}), s32[32,1,12]{2,1,0:T(1,128)S(1)}, u32[]{:S(2)}, u32[]{:S(2)}) %all-to-all-start.2) | async-done | bytes 1568 | tf_op jit(solution)/shard_map/all_to_all | solution.py:64
  46.1 6.5 %all-to-all-start.1 = ((bf16[32,12,1024]{2,1,0:T(8,128)(2,1)}), bf16[32,12,1024]{2,1,0:T(8,128)(2,1)}, u32[]{:S(2)}, u32[]{:S(2)}) async-start(bf16[32,12,1024]{2,1,0:T(8,128)(2,1)} %reshape.288), calls=%async_computation.1 | async-start | bytes 2097152 | tf_op jit(solution)/shard_map/all_to_all | solution.py:63
  54.1 54.2 %all-to-all-done.1 = bf16[32,12,1024]{2,1,0:T(8,128)(2,1)} async-done(((bf16[32,12,1024]{2,1,0:T(8,128)(2,1)}), bf16[32,12,1024]{2,1,0:T(8,128)(2,1)}, u32[]{:S(2)}, u32[]{:S(2)}) %all-to-all-start.1) | async-done | bytes 786464 | tf_op jit(solution)/shard_map/all_to_all | solution.py:63
  108.3 1.5 convert_reduce_fusion
  109.9 1.7 multiply_reduce_fusion
  111.7 2.4 %reshape.296 = f32[384,1024]{1,0:T(8,128)} reshape(bf16[32,12,1024]{2,1,0:T(8,128)(2,1)} %all-to-all-done.1) | data formatting | bytes 2359296 | tf_op jit(solution)/shard_map/convert_element_type | solution.py:21
  114.1 4.8 %multiply_convert_fusion = bf16[384,2048]{1,0:T(8,128)(2,1)S(1)} fusion(bf16[1024,2048]{1,0:T(8,128)(2,1)} %param.8, f32[384,1024]{1,0:T(8,128)} %reshape.296, f32[384]{0:T(512)S(1)} %rsqrt.20, f32[384]{0:T(512)S(1)} %div.23), kind=kOutput, calls=%fused_computation.3 | convolution fusion | flops 1615724544 | bytes 7343104 | tf_op jit(solution)/shard_map/dot_general | solution.py:22
  118.9 1.1 copy-done.2
  120.0 1.0 slice_bitcast_fusion.1
  122.0 3.0 %fusion.28 = (f32[384]{0:T(512)}, f32[4,128,384]{2,1,0:T(8,128)S(1)}) fusion(bf16[384,4,128]{0,2,1:T(8,128)(2,1)} %bitcast.50, pred[384,384]{1,0:T(8,128)(4,1)S(1)} %fusion.10, bf16[48,4,8,128]{3,2,1,0:T(8,128)(2,1)} %get-tuple-element.6, bf16[48,4,8,128]{3,2,1,0:T(8,128)(2,1)} %get-tuple-element.5), kind=kOutput, calls=%fused_computation.58 | convolution fusion | flops 306314880 | bytes 2115072 | tf_op jit(solution)/shard_map/hij,jhd->ihd/dot_general | solution.py:40
  125.8 1.2 copy.38
  127.0 2.2 %convolution_convert_fusion = bf16[384,1024]{1,0:T(8,128)(2,1)S(1)} fusion(bf16[512,1024]{1,0:T(8,128)(2,1)} %param.9, f32[384,512]{1,0:T(8,128)} %copy.38, bf16[384,2048]{1,0:T(8,128)(2,1)} %copy-done.2, f32[384]{0:T(512)S(1)} %add_rsqrt_fusion.1, f32[384]{0:T(512)S(1)} %broadcast_multiply_fusion.1), kind=kOutput, calls=%fused_computation.7 | convolution fusion | flops 404029440 | bytes 3017728 | tf_op jit(solution)/shard_map/dot_general | solution.py:74
  129.2 1.2 reshape.293
  130.5 4.8 %all-to-all-start.3 = ((bf16[32,12,1024]{2,1,0:T(8,128)(2,1)}), bf16[32,12,1024]{2,1,0:T(8,128)(2,1)}, u32[]{:S(2)}, u32[]{:S(2)}) async-start(bf16[32,12,1024]{2,1,0:T(8,128)(2,1)} %reshape.293), calls=%async_computation.3 | async-start | bytes 2097152 | tf_op jit(solution)/shard_map/all_to_all | solution.py:77
  135.5 55.6 %all-to-all-done.3 = bf16[32,12,1024]{2,1,0:T(8,128)(2,1)} async-done(((bf16[32,12,1024]{2,1,0:T(8,128)(2,1)}), bf16[32,12,1024]{2,1,0:T(8,128)(2,1)}, u32[]{:S(2)}, u32[]{:S(2)}) %all-to-all-start.3) | async-done | bytes 786464 | tf_op jit(solution)/shard_map/all_to_all | solution.py:77
  191.1 1.3 reshape.294
  192.4 2.0 gather_fusion.2
  194.4 2.0 %add_convert_fusion = bf16[256,1024]{1,0:T(8,128)(2,1)} fusion(bf16[256,1024]{1,0:T(8,128)(2,1)} %gather_fusion.2, bf16[256,1024]{1,0:T(8,128)(2,1)S(1)} %convolution_convert_fusion.1), kind=kLoop, calls=%fused_computation.15 | loop fusion | flops 1048576 | bytes 1572864 | tf_op jit(solution)/shard_map/convert_element_type | solution.py:81
  (43 shorter events, 8.8 us)
Async XLA Ops:
  0.0 35.3 %copy-start = (bf16[1024,1024]{1,0:T(8,128)(2,1)S(1)}, bf16[1024,1024]{1,0:T(8,128)(2,1)}, u32[]{:S(2)}) copy-start(bf16[1024,1024]{1,0:T(8,128)(2,1)} %param.7) | copy-start | bytes 6291460
  0.0 10.4 %copy-start.3 = (s32[1,32]{1,0:T(1,128)S(1)}, s32[1,32]{1,0:T(1,128)}, u32[]{:S(2)}) copy-start(s32[1,32]{1,0:T(1,128)} %param.10) | copy-start | bytes 388
  0.0 7.4 %copy-start.1 = (s32[256]{0:T(256)S(1)}, s32[256]{0:T(256)}, u32[]{:S(2)}) copy-start(s32[256]{0:T(256)} %param.11) | copy-start | bytes 3076
  0.0 11.9 %all-to-all-start = ((bf16[4,256,256]{2,1,0:T(8,128)(2,1)}), bf16[4,256,256]{2,1,0:T(8,128)(2,1)S(1)}, u32[]{:S(2)}, u32[]{:S(2)}) async-start(bf16[4,256,256]{2,1,0:T(8,128)(2,1)} %bitcast.49), calls=%async_computation | async-start | bytes 1048576 | tf_op jit(solution)/shard_map/all_to_all | solution.py:47
  5.9 1.4 copy-start.5
  11.9 34.2 %all-to-all-start.2 = ((s32[32,1,12]{2,1,0:T(1,128)}), s32[32,1,12]{2,1,0:T(1,128)S(1)}, u32[]{:S(2)}, u32[]{:S(2)}) async-start(s32[32,1,12]{2,1,0:T(1,128)} %bitcast.6), calls=%async_computation.2 | async-start | bytes 32768 | tf_op jit(solution)/shard_map/all_to_all | solution.py:64
  46.1 62.2 %all-to-all-start.1 = ((bf16[32,12,1024]{2,1,0:T(8,128)(2,1)}), bf16[32,12,1024]{2,1,0:T(8,128)(2,1)}, u32[]{:S(2)}, u32[]{:S(2)}) async-start(bf16[32,12,1024]{2,1,0:T(8,128)(2,1)} %reshape.288), calls=%async_computation.1 | async-start | bytes 2097152 | tf_op jit(solution)/shard_map/all_to_all | solution.py:63
  118.9 1.2 copy-start.2
  129.2 6.0 %copy-start.6 = (s32[32]{0:T(128)S(1)}, s32[32]{0:T(128)}, u32[]{:S(2)}) copy-start(s32[32]{0:T(128)} %copy-done.5) | copy-start | bytes 388
  129.2 6.1 %copy-start.4 = (s32[1,32]{1,0:T(1,128)S(1)}, s32[1,32]{1,0:T(1,128)}, u32[]{:S(2)}) copy-start(s32[1,32]{1,0:T(1,128)} %param.10) | copy-start | bytes 388
  130.5 60.6 %all-to-all-start.3 = ((bf16[32,12,1024]{2,1,0:T(8,128)(2,1)}), bf16[32,12,1024]{2,1,0:T(8,128)(2,1)}, u32[]{:S(2)}, u32[]{:S(2)}) async-start(bf16[32,12,1024]{2,1,0:T(8,128)(2,1)} %reshape.293), calls=%async_computation.3 | async-start | bytes 2097152 | tf_op jit(solution)/shard_map/all_to_all | solution.py:77
where the time goes:
time: 197 us; the launch traced here: 196 us
  waiting for transfers between devices  116 us (59%)
  starting transfers between devices  38.7 us (20%)
  local copies, waits for them, and re-layouts  19.9 us (10%)
  matrix products  11.8 us (6%)
  other arithmetic  9.3 us (5%)
    all_to_all x1, waiting for transfers between devices, on_device(): lax.all_to_all(branch.reshape(owners, capacity, -1), 'batch', split_axis=...  55.6 us
    all_to_all x1, waiting for transfers between devices, on_device(): lax.all_to_all(payload, 'batch', split_axis=0, concat_axis=0, tiled=True)  54.2 us
    all_to_all x1, starting transfers between devices, on_device(): lax.all_to_all(seg_send, 'batch', split_axis=0, concat_axis=0, tiled=True)  22.4 us
    all_to_all x1, starting transfers between devices, on_device(): lax.all_to_all(payload, 'batch', split_axis=0, concat_axis=0, tiled=True)  6.49 us
    all_to_all x1, waiting for transfers between devices, on_device(): lax.all_to_all(seg_send, 'batch', split_axis=0, concat_axis=0, tiled=True)  5.73 us
    all_to_all x1, starting transfers between devices, on_device(): lax.all_to_all(lookups, 'col', split_axis=0, concat_axis=1, tiled=True)  4.97 us
    all_to_all x1, starting transfers between devices, on_device(): lax.all_to_all(branch.reshape(owners, capacity, -1), 'batch', split_axis=...  4.8 us
    dot_general x1, matrix products, project(): jnp.dot(normed, joined_weight, preferred_element_type=jnp.float32)  4.79 us
  transfers between devices with their start and end apart: 4, of which 4 were waited for; matrix products, arithmetic and copies ran while one was open for 7% of the time, Pallas kernels for 0%

commit v1 on v0

v1 whole, which is shorter than its diff:
```python
import functools

import jax
import jax.numpy as jnp
from jax import lax
from jax.experimental import pallas as pl
from jax.experimental.pallas import tpu as pltpu
from jax.sharding import PartitionSpec as P

MESH = pl.DeviceIdType.MESH
HEADS = 4
HEAD_DIM = 128
WIDTH = HEADS * HEAD_DIM
D = 1024
CAP = 12
ROWS = 24
eps_norm = 1e-06
F32 = jnp.float32
BF16 = jnp.bfloat16

OFFSETS = [0] + [s * o for o in range(1, 8) for s in (1, -1)] + [8]
GROUPS = [(0, 6), (6, 10), (10, 14), (14, 16)]


def layer_norm(values):
    row_mean = jnp.mean(values, axis=-1, keepdims=True)
    centered = values - row_mean
    row_var = jnp.mean(centered * centered, axis=-1, keepdims=True)
    return centered * lax.rsqrt(row_var + eps_norm)


def silu(values):
    return values / (1.0 + jnp.exp(-values))


def dot(a, b):
    return jnp.dot(a, b, preferred_element_type=F32)


def dot_nt(a, b):
    return lax.dot_general(a, b, (((1,), (1,)), ((), ())), preferred_element_type=F32)


def iota(shape, dim):
    return lax.broadcasted_iota(jnp.int32, shape, dim)


def position(row, z, chips):
    a = row // ROWS
    i = row - a * ROWS
    step = (a + 1) // 2
    off = jnp.where((a & 1) == 1, step, chips - step)
    zz = z + off
    zz = jnp.where(zz >= chips, zz - chips, zz)
    zz = jnp.where(zz >= chips, zz - chips, zz)
    second = jnp.where(i < 16, i // 8, (i - 16) // 4)
    slot = jnp.where(i < 16, i & 7, 8 + (i & 3))
    return (2 * zz + second) * CAP + slot


def kernel(
    n, ncol, lk, win_h, wj_h, wo_h, cnt, usr, hid_o, br_o,
    tok, win, wj, wo, pay, rcv, sgp, sgr, joined, umat, mixed, rpay, rrcv,
    bar_x, wsem, lsem, xs, xr, gs, gr, fs, fr, bs, br,
):
    me = lax.axis_index("batch")
    col = lax.axis_index("col")
    chips = n // 2
    z, core = me // 2, lax.rem(me, 2)
    tokens = usr.shape[1]
    barrier = pltpu.get_barrier_semaphore()

    def sig_z(o, carry):
        pl.semaphore_signal(barrier, inc=1, device_id={"batch": lax.rem(me + o, n)}, device_id_type=MESH)
        return carry

    def sig_x(o, carry):
        pl.semaphore_signal(barrier, inc=1, device_id={"col": lax.rem(col + o, ncol)}, device_id_type=MESH)
        return carry

    lax.fori_loop(1, n, sig_z, 0)
    lax.fori_loop(1, ncol, sig_x, 0)

    weights = [
        pltpu.make_async_copy(win_h, win, wsem.at[0]),
        pltpu.make_async_copy(wj_h, wj, wsem.at[1]),
        pltpu.make_async_copy(wo_h, wo, wsem.at[2]),
    ]
    own_tok = pltpu.make_async_copy(lk.at[pl.ds(col * tokens, tokens)], tok.at[col], lsem.at[0])
    own_tok.start()
    for w in weights:
        w.start()

    counts = cnt[...].astype(F32)
    upto = (iota((n, n), 0) <= iota((n, n), 1)).astype(F32).astype(BF16)
    ends = dot(jnp.broadcast_to(counts, (8, n)).astype(BF16), upto)[0:1]
    starts = ends - counts
    rows = 8 * n
    row_d, row_r = iota((rows, n), 0) // 8, iota((rows, 1), 0) & 7
    mine = row_d == iota((rows, n), 1)
    start_col = jnp.sum(jnp.where(mine, starts, 0.0), axis=1, keepdims=True)
    count_col = jnp.sum(jnp.where(mine, counts, 0.0), axis=1, keepdims=True)
    lane_t = iota((rows, tokens), 1).astype(F32)
    first_r = row_r.astype(F32)
    last_r = 8.0 + (row_r & 3).astype(F32)
    pick_first = (lane_t == start_col + first_r) & (first_r < count_col)
    pick_last = (lane_t == start_col + last_r) & (last_r < count_col)
    users = usr[...].astype(F32) + 1.0
    seg_first = jnp.sum(jnp.where(pick_first, users, 0.0), axis=1, keepdims=True)
    seg_last = jnp.sum(jnp.where(pick_last, users, 0.0), axis=1, keepdims=True)
    lane = iota((rows, 128), 1)
    spread = jnp.where(lane == row_r, seg_first, 0.0) + jnp.where((lane == 8 + row_r) & (row_r < 4), seg_last, 0.0)
    own_rows = (iota((n, rows), 1) // 8 == iota((n, rows), 0)).astype(F32).astype(BF16)
    segs = dot(own_rows, spread.astype(BF16))
    for d in range(n):
        sgp[d] = segs[d : d + 1]

    pl.semaphore_wait(barrier, n - 1 + ncol - 1)

    def x_copy(o):
        peer = lax.rem(col + o, ncol)
        return pltpu.make_async_remote_copy(
            src_ref=lk.at[pl.ds(peer * tokens, tokens)], dst_ref=tok.at[col], send_sem=xs.at[o], recv_sem=xr.at[col],
            device_id={"col": peer}, device_id_type=MESH,
        )

    for o in range(1, ncol):
        x_copy(o).start()

    def z_copy(src, dst, send, recv, peer):
        return pltpu.make_async_remote_copy(
            src_ref=src.at[peer], dst_ref=dst.at[me], send_sem=send.at[peer], recv_sem=recv.at[me],
            device_id={"batch": peer}, device_id_type=MESH,
        )

    def z_wait(buf, send, recv, peer):
        pltpu.make_async_remote_copy(
            src_ref=buf.at[peer], dst_ref=buf.at[peer], send_sem=send.at[peer], recv_sem=recv.at[peer],
            device_id={"batch": peer}, device_id_type=MESH,
        ).wait_recv()

    partner = 2 * z + 1 - core

    def send_all(src, dst, send, recv):
        z_copy(src, dst, send, recv, partner).start()

        def step(o, carry):
            up, down = lax.rem(z + o, chips), lax.rem(z + chips - o, chips)
            for k in (0, 1):
                z_copy(src, dst, send, recv, 2 * up + k).start()
                z_copy(src, dst, send, recv, 2 * down + k).start()
            return carry

        lax.fori_loop(1, chips // 2, step, 0)
        across = lax.rem(z + chips // 2, chips)
        for k in (0, 1):
            z_copy(src, dst, send, recv, 2 * across + k).start()

    send_all(sgp, sgr, gs, gr)
    own_seg = pltpu.make_async_copy(sgp.at[me], sgr.at[me], lsem.at[1])
    own_seg.start()

    weights[0].wait()
    own_tok.wait()
    hidden = dot(tok[col], win[pl.ds(col * (D // ncol), D // ncol), :])
    for o in range(1, ncol):
        peer = lax.rem(col + o, ncol)
        pltpu.make_async_remote_copy(
            src_ref=tok.at[peer], dst_ref=tok.at[peer], send_sem=xs.at[o], recv_sem=xr.at[peer],
            device_id={"col": peer}, device_id_type=MESH,
        ).wait_recv()
        hidden += dot(tok[peer], win[pl.ds(peer * (D // ncol), D // ncol), :])
    hidden = hidden.astype(BF16)
    hid_o[...] = hidden

    first = dot(pick_first.astype(F32).astype(BF16), hidden)
    last = dot(pick_last.astype(F32).astype(BF16), hidden)
    pay[:, :, 0:D] = first.reshape(n, 8, D).astype(BF16)
    fold = jnp.where(row_r < 4, last[:, : D // 2], last[:, D // 2 :])
    pay[:, :, D:] = fold.reshape(n, 8, D // 2).astype(BF16)
    send_all(pay, rcv, fs, fr)
    own_pay = pltpu.make_async_copy(pay.at[me], rcv.at[me], lsem.at[2])
    own_pay.start()

    weights[1].wait()
    own_seg.wait()
    own_pay.wait()
    low = iota((8, 1), 0) < 4
    i24 = iota((ROWS, 128), 0)
    lane24 = iota((ROWS, 128), 1)
    want = jnp.where(i24 < 16, i24 & 7, 8 + (i24 & 3))
    is_a = (i24 < 8) | ((i24 >= 16) & (i24 < 20))

    for a0, a1 in GROUPS:
        parts = []
        for a in range(a0, a1):
            zz = lax.rem(z + (OFFSETS[a] + chips), chips)
            if a == 0:
                z_wait(sgr, gs, gr, partner)
                z_wait(rcv, fs, fr, partner)
            else:
                for k in (0, 1):
                    z_wait(sgr, gs, gr, 2 * zz + k)
                    z_wait(rcv, fs, fr, 2 * zz + k)
            va, vb = rcv[2 * zz].astype(F32), rcv[2 * zz + 1].astype(F32)
            ea, eb = va[:, D:], vb[:, D:]
            ex_lo = jnp.where(low, ea, pltpu.roll(eb, 4, 0))
            ex_hi = jnp.where(low, pltpu.roll(ea, 4, 0), eb)
            parts.append(jnp.concatenate([va[:, :D], vb[:, :D], jnp.concatenate([ex_lo, ex_hi], axis=1)], axis=0))
            seg = jnp.where(is_a, sgr[2 * zz], sgr[2 * zz + 1])
            seg = jnp.sum(jnp.where(lane24 == want, seg, 0.0), axis=1, keepdims=True)
            umat[a * ROWS : (a + 1) * ROWS, :] = jnp.where((lane24.astype(F32) == seg) & (lane24 > 0), 1.0, 0.0)
        r0, r1 = a0 * ROWS, a1 * ROWS
        normed = layer_norm(jnp.concatenate(parts, axis=0)).astype(BF16)

        def project(c, carry, normed=normed, r0=r0, r1=r1):
            cols = pl.ds(pl.multiple_of(c * WIDTH, WIDTH), WIDTH)
            joined[r0:r1, cols] = silu(dot(normed, wj[:, cols])).astype(BF16)
            return carry

        lax.fori_loop(0, 4, project, 0)

        u_all = umat[0:r1, :].astype(BF16)
        u_new = u_all[r0:r1]

        def allowed(ui, uj, i0, j0):
            shape = (ui.shape[0], uj.shape[0])
            pi = position(iota((shape[0], 1), 0) + i0, z, chips)
            pj = position(iota((1, shape[1]), 1) + j0, z, chips)
            return (dot_nt(ui, uj) > 0.5) & (pj <= pi)

        ok_new = allowed(u_all, u_new, 0, r0)
        ok_old = allowed(u_new, u_all[:r0], r0, 0) if r0 else None
        for h in range(HEADS):
            vs = slice(WIDTH + h * HEAD_DIM, WIDTH + (h + 1) * HEAD_DIM)
            qs = slice(2 * WIDTH + h * HEAD_DIM, 2 * WIDTH + (h + 1) * HEAD_DIM)
            ks = slice(3 * WIDTH + h * HEAD_DIM, 3 * WIDTH + (h + 1) * HEAD_DIM)
            hs = slice(h * HEAD_DIM, (h + 1) * HEAD_DIM)
            w = dot_nt(joined[0:r1, qs], joined[r0:r1, ks]) * HEAD_DIM ** (-0.5)
            w = jnp.where(ok_new, silu(w), 0.0).astype(BF16)
            add = dot(w, joined[r0:r1, vs])
            if r0:
                mixed[0:r0, hs] += add[:r0]
                w = dot_nt(joined[r0:r1, qs], joined[0:r0, ks]) * HEAD_DIM ** (-0.5)
                w = jnp.where(ok_old, silu(w), 0.0).astype(BF16)
                mixed[r0:r1, hs] = add[r0:] + dot(w, joined[0:r0, vs])
            else:
                mixed[0:r1, hs] = add

    for a0, a1 in GROUPS[::-1]:
        r0, r1 = a0 * ROWS, a1 * ROWS
        gated = layer_norm(mixed[r0:r1, :]) * joined[r0:r1, 0:WIDTH].astype(F32)
        for a in range(a0, a1)[::-1]:
            zz = lax.rem(z + (OFFSETS[a] + chips), chips)
            g = gated[(a - a0) * ROWS : (a - a0 + 1) * ROWS]
            e_lo, e_hi = g[16:24, : WIDTH // 2], g[16:24, WIDTH // 2 :]
            rpay[2 * zz, :, 0:WIDTH] = g[0:8].astype(BF16)
            rpay[2 * zz, :, WIDTH:] = jnp.where(low, e_lo, pltpu.roll(e_hi, 4, 0)).astype(BF16)
            rpay[2 * zz + 1, :, 0:WIDTH] = g[8:16].astype(BF16)
            rpay[2 * zz + 1, :, WIDTH:] = jnp.where(low, pltpu.roll(e_lo, 4, 0), e_hi).astype(BF16)
            if a == 0:
                z_copy(rpay, rrcv, bs, br, partner).start()
            else:
                for k in (0, 1):
                    z_copy(rpay, rrcv, bs, br, 2 * zz + k).start()
    own_ret = pltpu.make_async_copy(rpay.at[me], rrcv.at[me], lsem.at[3])
    own_ret.start()

    tok_t = iota((tokens, n), 0).astype(F32)
    dest = (tok_t >= starts) & (tok_t < ends)
    owner = jnp.sum(jnp.where(dest, iota((tokens, n), 1).astype(F32), 0.0), axis=1, keepdims=True)
    slot = jnp.sum(jnp.where(dest, tok_t - starts, 0.0), axis=1, keepdims=True)
    lane_p = iota((tokens, rows), 1)
    lane_i = lane_p & 7
    here = (lane_p // 8).astype(F32) == owner
    lane_f = lane_i.astype(F32)
    take_first = (here & (lane_f == slot)).astype(F32).astype(BF16)
    take_lo = (here & (lane_i < 4) & (lane_f + 8.0 == slot)).astype(F32).astype(BF16)
    take_hi = (here & (lane_i >= 4) & (lane_f + 4.0 == slot)).astype(F32).astype(BF16)

    own_ret.wait()
    weights[2].wait()

    def ret_wait(o, carry):
        z_wait(rrcv, bs, br, lax.rem(me + o, n))
        return carry

    lax.fori_loop(1, n, ret_wait, 0)
    back = rrcv[:, :, 0:WIDTH].astype(F32).reshape(rows, WIDTH).astype(BF16)
    back_x = rrcv[:, :, WIDTH:].astype(F32).reshape(rows, WIDTH // 2).astype(BF16)
    gated = dot(take_first, back)
    gated_lo = gated[:, : WIDTH // 2] + dot(take_lo, back_x)
    gated_hi = gated[:, WIDTH // 2 :] + dot(take_hi, back_x)
    branch = dot(gated_lo.astype(BF16), wo[: WIDTH // 2]) + dot(gated_hi.astype(BF16), wo[WIDTH // 2 :])
    br_o[...] = branch.astype(BF16)

    for o in range(1, ncol):
        x_copy(o).wait_send()

    def drain(o, carry):
        peer = lax.rem(me + o, n)
        z_copy(sgp, sgr, gs, gr, peer).wait_send()
        z_copy(pay, rcv, fs, fr, peer).wait_send()
        z_copy(rpay, rrcv, bs, br, peer).wait_send()
        return carry

    lax.fori_loop(1, n, drain, 0)


def on_device(n, ncol, lookups, input_weight, joined_weight, output_weight, owner_counts, user_index):
    tokens = user_index.shape[0]
    dma = pltpu.SemaphoreType.DMA
    anyspace = pl.BlockSpec(memory_space=pl.ANY)
    vmem = pl.BlockSpec(memory_space=pltpu.VMEM)
    hidden, branch = pl.pallas_call(
        functools.partial(kernel, n, ncol),
        name="hstu",
        out_shape=(jax.ShapeDtypeStruct((tokens, D), BF16), jax.ShapeDtypeStruct((tokens, D), BF16)),
        in_specs=[anyspace, anyspace, anyspace, anyspace, vmem, vmem],
        out_specs=(vmem, vmem),
        scratch_shapes=[
            pltpu.VMEM((ncol, tokens, D // ncol), BF16),
            pltpu.VMEM((D, D), BF16),
            pltpu.VMEM((D, 4 * WIDTH), BF16),
            pltpu.VMEM((WIDTH, D), BF16),
            pltpu.VMEM((n, 8, 3 * D // 2), BF16),
            pltpu.VMEM((n, 8, 3 * D // 2), BF16),
            pltpu.VMEM((n, 1, 128), F32),
            pltpu.VMEM((n, 1, 128), F32),
            pltpu.VMEM((n * CAP, 4 * WIDTH), BF16),
            pltpu.VMEM((n * CAP, 128), F32),
            pltpu.VMEM((n * CAP, WIDTH), F32),
            pltpu.VMEM((n, 8, 3 * WIDTH // 2), BF16),
            pltpu.VMEM((n, 8, 3 * WIDTH // 2), BF16),
            pltpu.SemaphoreType.REGULAR,
            dma((3,)), dma((4,)), dma((ncol,)), dma((ncol,)),
            dma((n,)), dma((n,)), dma((n,)), dma((n,)), dma((n,)), dma((n,)),
        ],
        compiler_params=pltpu.CompilerParams(collective_id=0, has_side_effects=True),
    )(lookups, input_weight, joined_weight, output_weight, owner_counts, user_index.reshape(1, tokens))
    return (hidden.astype(F32) + branch.astype(F32)).astype(BF16)


def solution(mesh):
    return jax.shard_map(
        functools.partial(on_device, mesh.shape["batch"], mesh.shape["col"]),
        mesh=mesh,
        in_specs=(
            P(("rep", "batch"), "col"),
            P(),
            P(),
            P(),
            P(("rep", "batch", "col"), None),
            P(("rep", "batch", "col")),
        ),
        out_specs=P(("rep", "batch", "col"), None),
        check_vma=False,
    )
```

time: 197 us -> 98.4 us (0.50)
  waiting for transfers between devices: 116 us -> 0 us
  Pallas kernels: 0 us -> 96 us
  starting transfers between devices: 38.7 us -> 0 us
  local copies, waits for them, and re-layouts: 19.9 us -> 0 us
  matrix products: 11.8 us -> 0 us
  other arithmetic: 9.3 us -> 2.19 us
    all_to_all x4 -> x0, waiting for transfers between devices: 116 us -> none  [the longest x1 55.6 us: on_device(): lax.all_to_all(branch.reshape(owners, capacity, -1), 'batch', split_axis=...]
    pallas_call x0 -> x1, Pallas kernels: none -> 96 us  [on_device(): pl.pallas_call(functools.partial(kernel, n, ncol), name='hstu', out_shape...]
    all_to_all x4 -> x0, starting transfers between devices: 38.7 us -> none  [the longest x1 22.4 us: on_device(): lax.all_to_all(seg_send, 'batch', split_axis=0, concat_axis=0, tiled=True)]
    dot_general x4 -> x0, matrix products: 11.8 us -> none  [the longest x1 4.79 us: project(): jnp.dot(normed, joined_weight, preferred_element_type=jnp.float32)]
    gather x4 -> x0, local copies, waits for them, and re-layouts: 6.94 us -> none  [the longest x2 2.9 us: on_device(): user_index[gather_rows]]
    reshape x6 -> x0, local copies, waits for them, and re-layouts: 6.52 us -> none  [the longest x1 1.31 us: on_device(): branch_rows = returned.reshape(owners * capacity, -1)[back_rows]]
    reduce_sum x5 -> x0, other arithmetic: 3.43 us -> none  [the longest x2 1.79 us: layer_norm(): row_var = jnp.mean(centered * centered, axis=-1, keepdims=True)]
    convert_element_type x1 -> x0, local copies, waits for them, and re-layouts: 2.36 us -> none  [project(): normed = layer_norm(hidden_rows.astype(jnp.float32)).astype(jnp.bfloat16)]
  transfers between devices with their start and end apart: 4 -> 0, of which waited for: 4 -> 0; matrix products, arithmetic and copies ran while one was open for 7% -> 0% of each run, Pallas kernels for 0% -> 0%
where the time goes in v1:
time: 98.4 us; the launch traced here: 98.2 us
  Pallas kernels  96 us (98%)
  other arithmetic  2.19 us (2%)
    pallas_call x1, Pallas kernels, on_device(): pl.pallas_call(functools.partial(kernel, n, ncol), name='hstu', out_shape...  96 us
    convert_element_type x1, other arithmetic, on_device(): return (hidden.astype(F32) + branch.astype(F32)).astype(BF16)  2.19 us

profile of v1, /device:TPU:1, one launch (start us, length us, event | category | flops | bytes accessed | tf_op | source)
XLA Modules:
  0.0 98.2 jit_solution(11871195972479853238)
XLA Ops:
  0.0 96.0 %hstu.1 = (bf16[256,1024]{1,0:T(8,128)(2,1)}, bf16[256,1024]{1,0:T(8,128)(2,1)}) custom-call(bf16[1024,256]{1,0:T(8,128)(2,1)} %lk.1, bf16[1024,1024]{1,0:T(8,128)(2,1)} %win_h.1, bf16[1024,2048]{1,0:T(8,128)(2,1)} %wj_h.1, bf16[512,1024]{1,0:T(8,128)(2,1)} %wo_h.1, s32[1,32]{1,0:T(1,128)} %cnt.1, s32[1,256]{1,0:T(1,128)} %bitcast.1), custom_call_target="tpu_custom_call" | custom-call | tf_op jit(solution)/shard_map/hstu/pallas_call | solution.py:315
  96.0 2.2 %add_convert_fusion = bf16[256,1024]{1,0:T(8,128)(2,1)} fusion(bf16[256,1024]{1,0:T(8,128)(2,1)} %get-tuple-element.8, bf16[256,1024]{1,0:T(8,128)(2,1)} %get-tuple-element.7), kind=kLoop, calls=%fused_computation | loop fusion | flops 1048576 | bytes 1572864 | tf_op jit(solution)/shard_map/convert_element_type | solution.py:341

commit v2 on v1

--- a/solution.py
+++ b/solution.py
@@ -19,6 +19,8 @@
 BF16 = jnp.bfloat16
 
 OFFSETS = [0] + [s * o for o in range(1, 8) for s in (1, -1)] + [8]
+REL = (0, 1, 3, 2)
+RING = [1, 2, 3, 4, 5, 6, 7, 8]
 GROUPS = [(0, 6), (6, 10), (10, 14), (14, 16)]
 
 
@@ -59,9 +61,9 @@
 
 
 def kernel(
-    n, ncol, lk, win_h, wj_h, wo_h, cnt, usr, hid_o, br_o,
+    n, ncol, lk, win_h, wj_h, wo_h, cnt, usr, out,
     tok, win, wj, wo, pay, rcv, sgp, sgr, joined, umat, mixed, rpay, rrcv,
-    bar_x, wsem, lsem, xs, xr, gs, gr, fs, fr, bs, br,
+    near2, near4, near8, wsem, lsem, xs, xr, gs, gr, fs, fr, bs, br,
 ):
     me = lax.axis_index("batch")
     col = lax.axis_index("col")
@@ -69,25 +71,32 @@
     z, core = me // 2, lax.rem(me, 2)
     tokens = usr.shape[1]
     barrier = pltpu.get_barrier_semaphore()
-
-    def sig_z(o, carry):
-        pl.semaphore_signal(barrier, inc=1, device_id={"batch": lax.rem(me + o, n)}, device_id_type=MESH)
-        return carry
-
-    def sig_x(o, carry):
+    partner = 2 * z + 1 - core
+    slab = D // ncol
+
+    def at(o):
+        return lax.rem(z + o + chips, chips)
+
+    def signal(sem, peer):
+        pl.semaphore_signal(sem, inc=1, device_id={"batch": peer}, device_id_type=MESH)
+
+    for o in range(1, ncol):
         pl.semaphore_signal(barrier, inc=1, device_id={"col": lax.rem(col + o, ncol)}, device_id_type=MESH)
-        return carry
-
-    lax.fori_loop(1, n, sig_z, 0)
-    lax.fori_loop(1, ncol, sig_x, 0)
-
+    signal(barrier, partner)
+    for o in (1, -1):
+        for k in (0, 1):
+            signal(barrier, 2 * at(o) + k)
+
+    own_tok = pltpu.make_async_copy(lk.at[pl.ds(col * tokens, tokens)], tok.at[0], lsem.at[0])
+    own_tok.start()
     weights = [
-        pltpu.make_async_copy(win_h, win, wsem.at[0]),
-        pltpu.make_async_copy(wj_h, wj, wsem.at[1]),
-        pltpu.make_async_copy(wo_h, wo, wsem.at[2]),
+        pltpu.make_async_copy(
+            win_h.at[pl.ds(lax.rem(col + REL[j], ncol) * slab, slab)], win.at[pl.ds(j * slab, slab)], wsem.at[j]
+        )
+        for j in range(ncol)
     ]
-    own_tok = pltpu.make_async_copy(lk.at[pl.ds(col * tokens, tokens)], tok.at[col], lsem.at[0])
-    own_tok.start()
+    weights.append(pltpu.make_async_copy(wj_h, wj, wsem.at[ncol]))
+    weights.append(pltpu.make_async_copy(wo_h, wo, wsem.at[ncol + 1]))
     for w in weights:
         w.start()
 
@@ -115,23 +124,42 @@
     for d in range(n):
         sgp[d] = segs[d : d + 1]
 
-    pl.semaphore_wait(barrier, n - 1 + ncol - 1)
+    pick_first = pick_first.astype(F32).astype(BF16)
+    pick_last = pick_last.astype(F32).astype(BF16)
+
+    def pack(j):
+        first = dot(pick_first, tok[j])
+        last = dot(pick_last, tok[j])
+        fold = jnp.where(row_r < 4, last[:, : slab // 2], last[:, slab // 2 :])
+        pay[:, j, :, 0:slab] = first.reshape(n, 8, slab).astype(BF16)
+        pay[:, j, :, slab:] = fold.reshape(n, 8, slab // 2).astype(BF16)
+
+    own_tok.wait()
+    pack(0)
+
+    pl.semaphore_wait(barrier, ncol - 1 + 5)
+    for o in (1, -1):
+        signal(near2, 2 * at(o) + core)
 
     def x_copy(o):
         peer = lax.rem(col + o, ncol)
+        j = REL.index(ncol - o)
         return pltpu.make_async_remote_copy(
-            src_ref=lk.at[pl.ds(peer * tokens, tokens)], dst_ref=tok.at[col], send_sem=xs.at[o], recv_sem=xr.at[col],
+            src_ref=lk.at[pl.ds(peer * tokens, tokens)], dst_ref=tok.at[j], send_sem=xs.at[o], recv_sem=xr.at[j],
             device_id={"col": peer}, device_id_type=MESH,
         )
 
     for o in range(1, ncol):
         x_copy(o).start()
 
-    def z_copy(src, dst, send, recv, peer):
+    def copy(src, dst, send, recv, peer):
         return pltpu.make_async_remote_copy(
-            src_ref=src.at[peer], dst_ref=dst.at[me], send_sem=send.at[peer], recv_sem=recv.at[me],
+            src_ref=src, dst_ref=dst, send_sem=send.at[peer], recv_sem=recv.at[me],
             device_id={"batch": peer}, device_id_type=MESH,
         )
+
+    def z_copy(src, dst, send, recv, peer):
+        return copy(src.at[peer], dst.at[me], send, recv, peer)
 
     def z_wait(buf, send, recv, peer):
         pltpu.make_async_remote_copy(
@@ -139,53 +167,57 @@
             device_id={"batch": peer}, device_id_type=MESH,
         ).wait_recv()
 
-    partner = 2 * z + 1 - core
-
-    def send_all(src, dst, send, recv):
-        z_copy(src, dst, send, recv, partner).start()
-
-        def step(o, carry):
-            up, down = lax.rem(z + o, chips), lax.rem(z + chips - o, chips)
+    def send_own(peer):
+        z_copy(sgp, sgr, gs, gr, peer).start()
+        copy(pay.at[peer, pl.ds(0, 1)], rcv.at[me, pl.ds(0, 1)], fs, fr, peer).start()
+
+    def send_rest(peer):
+        copy(pay.at[peer, pl.ds(1, ncol - 1)], rcv.at[me, pl.ds(1, ncol - 1)], fs, fr, peer).start()
+
+    def send_ring(send, offsets):
+        for o in offsets:
             for k in (0, 1):
-                z_copy(src, dst, send, recv, 2 * up + k).start()
-                z_copy(src, dst, send, recv, 2 * down + k).start()
-            return carry
-
-        lax.fori_loop(1, chips // 2, step, 0)
-        across = lax.rem(z + chips // 2, chips)
-        for k in (0, 1):
-            z_copy(src, dst, send, recv, 2 * across + k).start()
-
-    send_all(sgp, sgr, gs, gr)
+                send(2 * at(o) + k)
+                if 2 * o != chips:
+                    send(2 * at(-o) + k)
+
+    send_own(partner)
+    send_ring(send_own, [1])
+    pl.semaphore_wait(near2, 2)
+    for o in (2, -2):
+        signal(near4, 2 * at(o) + core)
+    send_ring(send_own, [2])
+    pl.semaphore_wait(near4, 2)
+    for o in (4, -4):
+        signal(near8, 2 * at(o) + core)
+    send_ring(send_own, [4, 3])
     own_seg = pltpu.make_async_copy(sgp.at[me], sgr.at[me], lsem.at[1])
     own_seg.start()
-
-    weights[0].wait()
-    own_tok.wait()
-    hidden = dot(tok[col], win[pl.ds(col * (D // ncol), D // ncol), :])
-    for o in range(1, ncol):
-        peer = lax.rem(col + o, ncol)
+    pl.semaphore_wait(near8, 2)
+    send_ring(send_own, [8, 7, 6, 5])
+
+    for j in range(1, ncol):
         pltpu.make_async_remote_copy(
-            src_ref=tok.at[peer], dst_ref=tok.at[peer], send_sem=xs.at[o], recv_sem=xr.at[peer],
-            device_id={"col": peer}, device_id_type=MESH,
+            src_ref=tok.at[j], dst_ref=tok.at[j], send_sem=xs.at[0], recv_sem=xr.at[j],
+            device_id={"col": lax.rem(col + 1, ncol)}, device_id_type=MESH,
         ).wait_recv()
-        hidden += dot(tok[peer], win[pl.ds(peer * (D // ncol), D // ncol), :])
-    hidden = hidden.astype(BF16)
-    hid_o[...] = hidden
-
-    first = dot(pick_first.astype(F32).astype(BF16), hidden)
-    last = dot(pick_last.astype(F32).astype(BF16), hidden)
-    pay[:, :, 0:D] = first.reshape(n, 8, D).astype(BF16)
-    fold = jnp.where(row_r < 4, last[:, : D // 2], last[:, D // 2 :])
-    pay[:, :, D:] = fold.reshape(n, 8, D // 2).astype(BF16)
-    send_all(pay, rcv, fs, fr)
+        pack(j)
+    send_rest(partner)
+    send_ring(send_rest, RING)
     own_pay = pltpu.make_async_copy(pay.at[me], rcv.at[me], lsem.at[2])
     own_pay.start()
 
-    weights[1].wait()
+    for w in weights[:ncol]:
+        w.wait()
+    hidden = dot(tok[0], win[0:slab])
+    for j in range(1, ncol):
+        hidden += dot(tok[j], win[j * slab : (j + 1) * slab])
+    hidden = hidden.astype(BF16)
+    weights[ncol].wait()
     own_seg.wait()
     own_pay.wait()
-    low = iota((8, 1), 0) < 4
+    low = iota((1, 8, 1), 1) < 4
+    low8 = iota((8, 1), 0) < 4
     i24 = iota((ROWS, 128), 0)
     lane24 = iota((ROWS, 128), 1)
     want = jnp.where(i24 < 16, i24 & 7, 8 + (i24 & 3))
@@ -203,15 +235,19 @@
                     z_wait(sgr, gs, gr, 2 * zz + k)
                     z_wait(rcv, fs, fr, 2 * zz + k)
             va, vb = rcv[2 * zz].astype(F32), rcv[2 * zz + 1].astype(F32)
-            ea, eb = va[:, D:], vb[:, D:]
-            ex_lo = jnp.where(low, ea, pltpu.roll(eb, 4, 0))
-            ex_hi = jnp.where(low, pltpu.roll(ea, 4, 0), eb)
-            parts.append(jnp.concatenate([va[:, :D], vb[:, :D], jnp.concatenate([ex_lo, ex_hi], axis=1)], axis=0))
+            ea, eb = va[:, :, slab:], vb[:, :, slab:]
+            ex_lo = jnp.where(low, ea, pltpu.roll(eb, 4, 1))
+            ex_hi = jnp.where(low, pltpu.roll(ea, 4, 1), eb)
+            parts.append(jnp.concatenate([v[:, :, :slab] for v in (va, vb)] + [jnp.concatenate([ex_lo, ex_hi], axis=2)], axis=1))
             seg = jnp.where(is_a, sgr[2 * zz], sgr[2 * zz + 1])
             seg = jnp.sum(jnp.where(lane24 == want, seg, 0.0), axis=1, keepdims=True)
             umat[a * ROWS : (a + 1) * ROWS, :] = jnp.where((lane24.astype(F32) == seg) & (lane24 > 0), 1.0, 0.0)
         r0, r1 = a0 * ROWS, a1 * ROWS
-        normed = layer_norm(jnp.concatenate(parts, axis=0)).astype(BF16)
+        looked = jnp.concatenate(parts, axis=1).astype(BF16)
+        projected = dot(looked[0], win[0:slab])
+        for j in range(1, ncol):
+            projected += dot(looked[j], win[j * slab : (j + 1) * slab])
+        normed = layer_norm(projected.astype(BF16).astype(F32)).astype(BF16)
 
         def project(c, carry, normed=normed, r0=r0, r1=r1):
             cols = pl.ds(pl.multiple_of(c * WIDTH, WIDTH), WIDTH)
@@ -255,9 +291,9 @@
             g = gated[(a - a0) * ROWS : (a - a0 + 1) * ROWS]
             e_lo, e_hi = g[16:24, : WIDTH // 2], g[16:24, WIDTH // 2 :]
             rpay[2 * zz, :, 0:WIDTH] = g[0:8].astype(BF16)
-            rpay[2 * zz, :, WIDTH:] = jnp.where(low, e_lo, pltpu.roll(e_hi, 4, 0)).astype(BF16)
+            rpay[2 * zz, :, WIDTH:] = jnp.where(low8, e_lo, pltpu.roll(e_hi, 4, 0)).astype(BF16)
             rpay[2 * zz + 1, :, 0:WIDTH] = g[8:16].astype(BF16)
-            rpay[2 * zz + 1, :, WIDTH:] = jnp.where(low, pltpu.roll(e_lo, 4, 0), e_hi).astype(BF16)
+            rpay[2 * zz + 1, :, WIDTH:] = jnp.where(low8, pltpu.roll(e_lo, 4, 0), e_hi).astype(BF16)
             if a == 0:
                 z_copy(rpay, rrcv, bs, br, partner).start()
             else:
@@ -279,7 +315,7 @@
     take_hi = (here & (lane_i >= 4) & (lane_f + 4.0 == slot)).astype(F32).astype(BF16)
 
     own_ret.wait()
-    weights[2].wait()
+    weights[ncol + 1].wait()
 
     def ret_wait(o, carry):
         z_wait(rrcv, bs, br, lax.rem(me + o, n))
@@ -292,7 +328,7 @@
     gated_lo = gated[:, : WIDTH // 2] + dot(take_lo, back_x)
     gated_hi = gated[:, WIDTH // 2 :] + dot(take_hi, back_x)
     branch = dot(gated_lo.astype(BF16), wo[: WIDTH // 2]) + dot(gated_hi.astype(BF16), wo[WIDTH // 2 :])
-    br_o[...] = branch.astype(BF16)
+    out[...] = (hidden.astype(F32) + branch.astype(BF16).astype(F32)).astype(BF16)
 
     for o in range(1, ncol):
         x_copy(o).wait_send()
@@ -300,7 +336,7 @@
     def drain(o, carry):
         peer = lax.rem(me + o, n)
         z_copy(sgp, sgr, gs, gr, peer).wait_send()
-        z_copy(pay, rcv, fs, fr, peer).wait_send()
+        copy(pay.at[peer], rcv.at[me], fs, fr, peer).wait_send()
         z_copy(rpay, rrcv, bs, br, peer).wait_send()
         return carry
 
@@ -312,19 +348,19 @@
     dma = pltpu.SemaphoreType.DMA
     anyspace = pl.BlockSpec(memory_space=pl.ANY)
     vmem = pl.BlockSpec(memory_space=pltpu.VMEM)
-    hidden, branch = pl.pallas_call(
+    return pl.pallas_call(
         functools.partial(kernel, n, ncol),
         name="hstu",
-        out_shape=(jax.ShapeDtypeStruct((tokens, D), BF16), jax.ShapeDtypeStruct((tokens, D), BF16)),
+        out_shape=jax.ShapeDtypeStruct((tokens, D), BF16),
         in_specs=[anyspace, anyspace, anyspace, anyspace, vmem, vmem],
-        out_specs=(vmem, vmem),
+        out_specs=vmem,
         scratch_shapes=[
             pltpu.VMEM((ncol, tokens, D // ncol), BF16),
             pltpu.VMEM((D, D), BF16),
             pltpu.VMEM((D, 4 * WIDTH), BF16),
             pltpu.VMEM((WIDTH, D), BF16),
-            pltpu.VMEM((n, 8, 3 * D // 2), BF16),
-            pltpu.VMEM((n, 8, 3 * D // 2), BF16),
+            pltpu.VMEM((n, ncol, 8, 3 * D // 2 // ncol), BF16),
+            pltpu.VMEM((n, ncol, 8, 3 * D // 2 // ncol), BF16),
             pltpu.VMEM((n, 1, 128), F32),
             pltpu.VMEM((n, 1, 128), F32),
             pltpu.VMEM((n * CAP, 4 * WIDTH), BF16),
@@ -332,13 +368,12 @@
             pltpu.VMEM((n * CAP, WIDTH), F32),
             pltpu.VMEM((n, 8, 3 * WIDTH // 2), BF16),
             pltpu.VMEM((n, 8, 3 * WIDTH // 2), BF16),
-            pltpu.SemaphoreType.REGULAR,
-            dma((3,)), dma((4,)), dma((ncol,)), dma((ncol,)),
+            pltpu.SemaphoreType.REGULAR, pltpu.SemaphoreType.REGULAR, pltpu.SemaphoreType.REGULAR,
+            dma((ncol + 2,)), dma((4,)), dma((ncol,)), dma((ncol,)),
             dma((n,)), dma((n,)), dma((n,)), dma((n,)), dma((n,)), dma((n,)),
         ],
         compiler_params=pltpu.CompilerParams(collective_id=0, has_side_effects=True),
     )(lookups, input_weight, joined_weight, output_weight, owner_counts, user_index.reshape(1, tokens))
-    return (hidden.astype(F32) + branch.astype(F32)).astype(BF16)
 
 
 def solution(mesh):

time: 98.4 us -> 90.2 us (0.917)
  Pallas kernels: 96 us -> 88.2 us
  other arithmetic: 2.19 us -> 0 us
  local copies, waits for them, and re-layouts: 0 us -> 1.87 us
    pallas_call x1, Pallas kernels: 96 us -> 88.2 us  [on_device(): pl.pallas_call(functools.partial(kernel, n, ncol), name='hstu', out_shape...]
    convert_element_type x1 -> x0, other arithmetic: 2.19 us -> none  [on_device(): return (hidden.astype(F32) + branch.astype(F32)).astype(BF16)]
    unnamed x0 -> x1, local copies, waits for them, and re-layouts: none -> 1.87 us
where the time goes in v2:
time: 90.2 us; the launch traced here: 90 us
  Pallas kernels  88.2 us (98%)
  local copies, waits for them, and re-layouts  1.87 us (2%)
    pallas_call x1, Pallas kernels, on_device(): pl.pallas_call(functools.partial(kernel, n, ncol), name='hstu', out_shape...  88.2 us
    unnamed x1, local copies, waits for them, and re-layouts  1.87 us

profile of v2, /device:TPU:1, one launch (start us, length us, event | category | flops | bytes accessed | tf_op | source)
XLA Modules:
  0.0 90.0 jit_solution(10027935750024475549)
XLA Ops:
  0.0 88.2 %hstu.1 = bf16[256,1024]{1,0:T(8,128)(2,1)} custom-call(bf16[1024,256]{1,0:T(8,128)(2,1)} %lk.1, bf16[1024,1024]{1,0:T(8,128)(2,1)} %win_h.1, bf16[1024,2048]{1,0:T(8,128)(2,1)} %wj_h.1, bf16[512,1024]{1,0:T(8,128)(2,1)} %wo_h.1, s32[1,32]{1,0:T(1,128)} %cnt.1, s32[1,256]{1,0:T(1,128)} %bitcast.1), custom_call_target="tpu_custom_call" | custom-call | tf_op jit(solution)/shard_map/hstu/pallas_call | solution.py:351
  88.2 1.9 %copy.8 = bf16[256,1024]{1,0:T(8,128)(2,1)} copy(bf16[256,1024]{1,0:T(8,128)(2,1)} %hstu.1) | data formatting | bytes 1048576

commit v3 on v2

v3 whole, which is shorter than its diff:
```python
import functools

import jax
import jax.numpy as jnp
from jax import lax
from jax.experimental import pallas as pl
from jax.experimental.pallas import tpu as pltpu
from jax.sharding import PartitionSpec as P

MESH = pl.DeviceIdType.MESH
HEADS = 4
HEAD_DIM = 128
WIDTH = HEADS * HEAD_DIM
D = 1024
CAP = 12
ROWS = 24
eps_norm = 1e-06
F32 = jnp.float32
BF16 = jnp.bfloat16

OFFSETS = [0, 8] + [s * o for o in range(7, 0, -1) for s in (1, -1)]
REL = (0, 1, 3, 2)
GROUPS = [(0, 6), (6, 10), (10, 16)]


def group_of(o):
    a = OFFSETS.index(abs(o))
    return [a0 <= a < a1 for a0, a1 in GROUPS].index(True)


def layer_norm(values):
    row_mean = jnp.mean(values, axis=-1, keepdims=True)
    centered = values - row_mean
    row_var = jnp.mean(centered * centered, axis=-1, keepdims=True)
    return centered * lax.rsqrt(row_var + eps_norm)


def silu(values, scale=1.0):
    half = values * (0.5 * scale)
    return half + half * jnp.tanh(half)


def dot(a, b):
    return jnp.dot(a, b, preferred_element_type=F32)


def dot_nt(a, b):
    return lax.dot_general(a, b, (((1,), (1,)), ((), ())), preferred_element_type=F32)


def iota(shape, dim):
    return lax.broadcasted_iota(jnp.int32, shape, dim)


def position(row, z, chips):
    a = row // ROWS
    i = row - a * ROWS
    step = jnp.where(a == 0, 0, chips // 2 - a // 2)
    off = jnp.where((a & 1) == 1, chips - step, step)
    zz = z + off
    zz = jnp.where(zz >= chips, zz - chips, zz)
    zz = jnp.where(zz >= chips, zz - chips, zz)
    second = jnp.where(i < 16, i // 8, (i - 16) // 4)
    slot = jnp.where(i < 16, i & 7, 8 + (i & 3))
    return (2 * zz + second) * CAP + slot


def kernel(
    n, ncol, lk, win_h, wj_h, wo_h, cnt_h, usr_h, out,
    cnt, usr, tok, win, wj, wo, pay, rcv, sgp, sgr, joined, umat, okm, mixed, rpay, rrcv,
    near2, near4, near8, wsem, lsem, xs, xr, gs, gr, fs, fr, bs, br,
):
    me = lax.axis_index("batch")
    col = lax.axis_index("col")
    chips = n // 2
    z, core = me // 2, lax.rem(me, 2)
    tokens = usr.shape[1]
    barrier = pltpu.get_barrier_semaphore()
    partner = 2 * z + 1 - core
    slab = D // ncol

    def at(o):
        return lax.rem(z + o + chips, chips)

    def signal(sem, peer):
        pl.semaphore_signal(sem, inc=1, device_id={"batch": peer}, device_id_type=MESH)

    for o in range(1, ncol):
        pl.semaphore_signal(barrier, inc=1, device_id={"col": lax.rem(col + o, ncol)}, device_id_type=MESH)
    signal(barrier, partner)
    for o in (1, -1):
        for k in (0, 1):
            signal(barrier, 2 * at(o) + k)

    small = [pltpu.make_async_copy(cnt_h, cnt, lsem.at[4]), pltpu.make_async_copy(usr_h, usr, lsem.at[5])]
    for c in small:
        c.start()
    own_tok = pltpu.make_async_copy(lk.at[pl.ds(col * tokens, tokens)], tok.at[0], lsem.at[0])
    own_tok.start()
    weights = [
        pltpu.make_async_copy(
            win_h.at[pl.ds(lax.rem(col + REL[j], ncol) * slab, slab)], win.at[pl.ds(j * slab, slab)], wsem.at[0]
        )
        for j in range(ncol)
    ]
    weights.append(pltpu.make_async_copy(wj_h, wj, wsem.at[1]))
    weights.append(pltpu.make_async_copy(wo_h, wo, wsem.at[2]))
    for w in weights:
        w.start()

    def x_copy(o):
        peer = lax.rem(col + o, ncol)
        j = REL.index(ncol - o)
        return pltpu.make_async_remote_copy(
            src_ref=lk.at[pl.ds(peer * tokens, tokens)], dst_ref=tok.at[j], send_sem=xs, recv_sem=xr,
            device_id={"col": peer}, device_id_type=MESH,
        )

    pl.semaphore_wait(barrier, ncol - 1 + 5)
    for o in (1, -1):
        signal(near2, 2 * at(o) + core)
    for o in range(1, ncol):
        x_copy(o).start()

    for c in small:
        c.wait()
    counts = cnt[...].astype(F32)
    upto = (iota((n, n), 0) <= iota((n, n), 1)).astype(F32).astype(BF16)
    ends = dot(jnp.broadcast_to(counts, (8, n)).astype(BF16), upto)[0:1]
    starts = ends - counts
    rows = 8 * n
    row_d, row_r = iota((rows, n), 0) // 8, iota((rows, 1), 0) & 7
    mine = row_d == iota((rows, n), 1)
    start_col = jnp.sum(jnp.where(mine, starts, 0.0), axis=1, keepdims=True)
    count_col = jnp.sum(jnp.where(mine, counts, 0.0), axis=1, keepdims=True)

    pl.semaphore_wait(near2, 2)
    for o in (2, -2):
        signal(near4, 2 * at(o) + core)

    lane_t = iota((rows, tokens), 1).astype(F32)
    first_r = row_r.astype(F32)
    last_r = 8.0 + (row_r & 3).astype(F32)
    want_first = jnp.where(first_r < count_col, start_col + first_r, -1.0)
    want_last = jnp.where(last_r < count_col, start_col + last_r, -1.0)
    is_first = lane_t == want_first
    is_last = lane_t == want_last
    pick_first = is_first.astype(F32).astype(BF16)
    pick_last = is_last.astype(F32).astype(BF16)

    def pack(j):
        first = dot(pick_first, tok[j])
        last = dot(pick_last, tok[j])
        fold = jnp.where(row_r < 4, last[:, : slab // 2], last[:, slab // 2 :])
        pay[:, j, :, 0:slab] = first.reshape(n, 8, slab).astype(BF16)
        pay[:, j, :, slab:] = fold.reshape(n, 8, slab // 2).astype(BF16)

    own_tok.wait()
    pack(0)

    def copy(src, dst, send, recv, peer):
        return pltpu.make_async_remote_copy(
            src_ref=src, dst_ref=dst, send_sem=send, recv_sem=recv, device_id={"batch": peer}, device_id_type=MESH
        )

    def whole(buf, blocks, send, recv):
        return copy(buf.at[pl.ds(0, blocks)], buf.at[pl.ds(0, blocks)], send, recv, partner)

    def send_own(peer, o):
        copy(pay.at[peer, pl.ds(0, 1)], rcv.at[me, pl.ds(0, 1)], fs, fr.at[group_of(o)], peer).start()

    def send_rest(peer, o):
        copy(pay.at[peer, pl.ds(1, ncol - 1)], rcv.at[me, pl.ds(1, ncol - 1)], fs, fr.at[group_of(o)], peer).start()

    def send_seg(peer, o):
        copy(sgp.at[peer], sgr.at[me], gs, gr, peer).start()

    def send_back(peer, o):
        copy(rpay.at[peer], rrcv.at[me], bs, br, peer).start()

    def send_ring(send, offsets):
        for o in offsets:
            for k in (0, 1):
                send(2 * at(o) + k, o)
                if 2 * o != chips:
                    send(2 * at(-o) + k, o)

    send_own(partner, 0)
    send_ring(send_own, [2, 1])
    pl.semaphore_wait(near4, 2)
    for o in (4, -4):
        signal(near8, 2 * at(o) + core)
    send_ring(send_own, [4, 3])

    users = usr[...].astype(F32) + 1.0
    seg_first = jnp.sum(jnp.where(is_first, users, 0.0), axis=1, keepdims=True)
    seg_last = jnp.sum(jnp.where(is_last, users, 0.0), axis=1, keepdims=True)
    lane = iota((rows, 128), 1)
    spread = jnp.where(lane == row_r, seg_first, 0.0) + jnp.where((lane == 8 + row_r) & (row_r < 4), seg_last, 0.0)
    own_rows = (iota((n, rows), 1) // 8 == iota((n, rows), 0)).astype(F32).astype(BF16)
    segs = dot(own_rows, spread.astype(BF16))
    for d in range(n):
        sgp[d] = segs[d : d + 1]

    pl.semaphore_wait(near8, 2)
    send_ring(send_own, [8, 7, 6, 5])
    send_seg(partner, 0)
    send_ring(send_seg, range(chips // 2, 0, -1))
    own_seg = pltpu.make_async_copy(sgp.at[me], sgr.at[me], lsem.at[1])
    own_seg.start()

    pltpu.make_async_remote_copy(
        src_ref=tok.at[pl.ds(1, ncol - 1)], dst_ref=tok.at[pl.ds(1, ncol - 1)], send_sem=xs, recv_sem=xr,
        device_id={"col": lax.rem(col + 1, ncol)}, device_id_type=MESH,
    ).wait_recv()
    for j in range(1, ncol):
        pack(j)
    send_rest(partner, 0)
    send_ring(send_rest, range(chips // 2, 0, -1))
    own_pay = pltpu.make_async_copy(pay.at[me], rcv.at[me], lsem.at[2])
    own_pay.start()

    pltpu.make_async_copy(win_h, win, wsem.at[0]).wait()
    hidden = dot(tok[0], win[0:slab])
    for j in range(1, ncol):
        hidden += dot(tok[j], win[j * slab : (j + 1) * slab])
    hidden = hidden.astype(BF16)

    low = iota((1, 8, 1), 1) < 4
    low8 = iota((8, 1), 0) < 4
    i24 = iota((ROWS, 128), 0)
    lane24 = iota((ROWS, 128), 1)
    want = jnp.where(i24 < 16, i24 & 7, 8 + (i24 & 3))
    is_a = (i24 < 8) | ((i24 >= 16) & (i24 < 20))
    own_seg.wait()
    whole(sgr, n - 1, gs, gr).wait_recv()
    for a in range(chips):
        zz = at(OFFSETS[a])
        seg = jnp.where(is_a, sgr[2 * zz], sgr[2 * zz + 1])
        seg = jnp.sum(jnp.where(lane24 == want, seg, 0.0), axis=1, keepdims=True)
        umat[a * ROWS : (a + 1) * ROWS, :] = jnp.where((lane24.astype(F32) == seg) & (lane24 > 0), 1.0, 0.0)
    slots = n * CAP
    users_all = umat[...].astype(BF16)
    pos_j = position(iota((1, slots), 1), z, chips)
    for a in range(0, chips, 4):
        part = slice(a * ROWS, (a + 4) * ROWS)
        pos_i = position(iota((4 * ROWS, 1), 0) + a * ROWS, z, chips)
        same = dot_nt(umat[part, :].astype(BF16), users_all) > 0.5
        okm[part, :] = jnp.where(same & (pos_j <= pos_i), 1.0, 0.0)

    weights[ncol].wait()
    own_pay.wait()
    for g, (a0, a1) in enumerate(GROUPS):
        whole(rcv, 2 * (a1 - a0) - (a0 == 0), fs, fr.at[g]).wait_recv()
        parts = []
        for a in range(a0, a1):
            zz = at(OFFSETS[a])
            va, vb = rcv[2 * zz].astype(F32), rcv[2 * zz + 1].astype(F32)
            ea, eb = va[:, :, slab:], vb[:, :, slab:]
            ex_lo = jnp.where(low, ea, pltpu.roll(eb, 4, 1))
            ex_hi = jnp.where(low, pltpu.roll(ea, 4, 1), eb)
            parts.append(jnp.concatenate([v[:, :, :slab] for v in (va, vb)] + [jnp.concatenate([ex_lo, ex_hi], axis=2)], axis=1))
        r0, r1 = a0 * ROWS, a1 * ROWS
        looked = jnp.concatenate(parts, axis=1).astype(BF16)
        projected = dot(looked[0], win[0:slab])
        for j in range(1, ncol):
            projected += dot(looked[j], win[j * slab : (j + 1) * slab])
        normed = layer_norm(projected.astype(BF16).astype(F32)).astype(BF16)

        def project(c, carry, normed=normed, r0=r0, r1=r1):
            cols = pl.ds(pl.multiple_of(c * WIDTH, WIDTH), WIDTH)
            joined[r0:r1, cols] = silu(dot(normed, wj[:, cols])).astype(BF16)
            return carry

        lax.fori_loop(0, 4, project, 0)

        for h in range(HEADS):
            vs = slice(WIDTH + h * HEAD_DIM, WIDTH + (h + 1) * HEAD_DIM)
            qs = slice(2 * WIDTH + h * HEAD_DIM, 2 * WIDTH + (h + 1) * HEAD_DIM)
            ks = slice(3 * WIDTH + h * HEAD_DIM, 3 * WIDTH + (h + 1) * HEAD_DIM)
            hs = slice(h * HEAD_DIM, (h + 1) * HEAD_DIM)
            w = silu(dot_nt(joined[0:r1, qs], joined[r0:r1, ks]), HEAD_DIM ** (-0.5))
            add = dot((w * okm[0:r1, r0:r1]).astype(BF16), joined[r0:r1, vs])
            if r0:
                mixed[0:r0, hs] += add[:r0]
                w = silu(dot_nt(joined[r0:r1, qs], joined[0:r0, ks]), HEAD_DIM ** (-0.5))
                mixed[r0:r1, hs] = add[r0:] + dot((w * okm[r0:r1, 0:r0]).astype(BF16), joined[0:r0, vs])
            else:
                mixed[0:r1, hs] = add

    for a0 in range(0, chips, 2):
        gated = layer_norm(mixed[a0 * ROWS : (a0 + 2) * ROWS, :]) * joined[a0 * ROWS : (a0 + 2) * ROWS, 0:WIDTH].astype(F32)
        for a in (a0 + 1, a0):
            zz = at(OFFSETS[a])
            g = gated[(a - a0) * ROWS : (a - a0 + 1) * ROWS]
            e_lo, e_hi = g[16:24, : WIDTH // 2], g[16:24, WIDTH // 2 :]
            rpay[2 * zz, :, 0:WIDTH] = g[0:8].astype(BF16)
            rpay[2 * zz, :, WIDTH:] = jnp.where(low8, e_lo, pltpu.roll(e_hi, 4, 0)).astype(BF16)
            rpay[2 * zz + 1, :, 0:WIDTH] = g[8:16].astype(BF16)
            rpay[2 * zz + 1, :, WIDTH:] = jnp.where(low8, pltpu.roll(e_lo, 4, 0), e_hi).astype(BF16)
            if a == 0:
                send_back(partner, 0)
            else:
                for k in (0, 1):
                    send_back(2 * zz + k, OFFSETS[a])
    own_ret = pltpu.make_async_copy(rpay.at[me], rrcv.at[me], lsem.at[3])
    own_ret.start()

    tok_t = iota((tokens, n), 0).astype(F32)
    dest = (tok_t >= starts) & (tok_t < ends)
    owner = jnp.sum(jnp.where(dest, iota((tokens, n), 1).astype(F32), 0.0), axis=1, keepdims=True)
    slot = jnp.sum(jnp.where(dest, tok_t - starts, 0.0), axis=1, keepdims=True)
    lane_p = iota((tokens, rows), 1)
    lane_i = lane_p & 7
    here = (lane_p // 8).astype(F32) == owner
    lane_f = lane_i.astype(F32)
    take_first = (here & (lane_f == slot)).astype(F32).astype(BF16)
    take_lo = (here & (lane_i < 4) & (lane_f + 8.0 == slot)).astype(F32).astype(BF16)
    take_hi = (here & (lane_i >= 4) & (lane_f + 4.0 == slot)).astype(F32).astype(BF16)

    pltpu.make_async_remote_copy(
        src_ref=tok.at[pl.ds(1, ncol - 1)], dst_ref=tok.at[pl.ds(1, ncol - 1)], send_sem=xs, recv_sem=xr,
        device_id={"col": lax.rem(col + 1, ncol)}, device_id_type=MESH,
    ).wait_send()
    whole(sgp, n - 1, gs, gr).wait_send()
    whole(pay, n - 1, fs, fr.at[0]).wait_send()
    own_ret.wait()
    weights[ncol + 1].wait()

    whole(rrcv, n - 1, bs, br).wait_recv()
    back = rrcv[:, :, 0:WIDTH].astype(F32).reshape(rows, WIDTH).astype(BF16)
    back_x = rrcv[:, :, WIDTH:].astype(F32).reshape(rows, WIDTH // 2).astype(BF16)
    gated = dot(take_first, back)
    gated_lo = gated[:, : WIDTH // 2] + dot(take_lo, back_x)
    gated_hi = gated[:, WIDTH // 2 :] + dot(take_hi, back_x)
    branch = dot(gated_lo.astype(BF16), wo[: WIDTH // 2]) + dot(gated_hi.astype(BF16), wo[WIDTH // 2 :])
    out[...] = (hidden.astype(F32) + branch.astype(BF16).astype(F32)).astype(BF16)

    whole(rpay, n - 1, bs, br).wait_send()


def on_device(n, ncol, lookups, input_weight, joined_weight, output_weight, owner_counts, user_index):
    tokens = user_index.shape[0]
    dma = pltpu.SemaphoreType.DMA
    anyspace = pl.BlockSpec(memory_space=pl.ANY)
    vmem = pl.BlockSpec(memory_space=pltpu.VMEM)
    return pl.pallas_call(
        functools.partial(kernel, n, ncol),
        name="hstu",
        out_shape=pltpu.VMEM((tokens, D), BF16),
        in_specs=[anyspace] * 6,
        out_specs=vmem,
        scratch_shapes=[
            pltpu.VMEM((1, n), jnp.int32),
            pltpu.VMEM((1, tokens), jnp.int32),
            pltpu.VMEM((ncol, tokens, D // ncol), BF16),
            pltpu.VMEM((D, D), BF16),
            pltpu.VMEM((D, 4 * WIDTH), BF16),
            pltpu.VMEM((WIDTH, D), BF16),
            pltpu.VMEM((n, ncol, 8, 3 * D // 2 // ncol), BF16),
            pltpu.VMEM((n, ncol, 8, 3 * D // 2 // ncol), BF16),
            pltpu.VMEM((n, 1, 128), F32),
            pltpu.VMEM((n, 1, 128), F32),
            pltpu.VMEM((n * CAP, 4 * WIDTH), BF16),
            pltpu.VMEM((n * CAP, 128), F32),
            pltpu.VMEM((n * CAP, n * CAP), F32),
            pltpu.VMEM((n * CAP, WIDTH), F32),
            pltpu.VMEM((n, 8, 3 * WIDTH // 2), BF16),
            pltpu.VMEM((n, 8, 3 * WIDTH // 2), BF16),
            pltpu.SemaphoreType.REGULAR, pltpu.SemaphoreType.REGULAR, pltpu.SemaphoreType.REGULAR,
            dma((3,)), dma((6,)), dma, dma, dma, dma, dma, dma((len(GROUPS),)), dma, dma,
        ],
        compiler_params=pltpu.CompilerParams(collective_id=0, has_side_effects=True),
    )(lookups, input_weight, joined_weight, output_weight, owner_counts, user_index.reshape(1, tokens))


def solution(mesh):
    return jax.shard_map(
        functools.partial(on_device, mesh.shape["batch"], mesh.shape["col"]),
        mesh=mesh,
        in_specs=(
            P(("rep", "batch"), "col"),
            P(),
            P(),
            P(),
            P(("rep", "batch", "col"), None),
            P(("rep", "batch", "col")),
        ),
        out_specs=P(("rep", "batch", "col"), None),
        check_vma=False,
    )
```

time: 90.2 us -> 83.1 us (0.921)
  Pallas kernels: 88.2 us -> 82.2 us
  local copies, waits for them, and re-layouts: 1.87 us -> 0.8 us
    pallas_call x1, Pallas kernels: 88.2 us -> 82.2 us  [on_device(): pl.pallas_call(functools.partial(kernel, n, ncol), name='hstu', out_shape...]
    unnamed x1, local copies, waits for them, and re-layouts: 1.87 us -> 0.8 us
where the time goes in v3:
time: 83.1 us; the launch traced here: 83 us
  Pallas kernels  82.2 us (99%)
    pallas_call x1, Pallas kernels, on_device(): pl.pallas_call(functools.partial(kernel, n, ncol), name='hstu', out_shape...  82.2 us

profile of v3, /device:TPU:1, one launch (start us, length us, event | category | flops | bytes accessed | tf_op | source)
XLA Modules:
  0.0 83.0 jit_solution(3545133718643962067)
XLA Ops:
  0.0 82.2 %hstu.1 = bf16[256,1024]{1,0:T(8,128)(2,1)S(1)} custom-call(bf16[1024,256]{1,0:T(8,128)(2,1)} %lk.1, bf16[1024,1024]{1,0:T(8,128)(2,1)} %win_h.1, bf16[1024,2048]{1,0:T(8,128)(2,1)} %wj_h.1, bf16[512,1024]{1,0:T(8,128)(2,1)} %wo_h.1, s32[1,32]{1,0:T(1,128)} %cnt_h.1, s32[1,256]{1,0:T(1,128)} %bitcast.1), custom_call_target="tpu_custom_call" | custom-call | tf_op jit(solution)/shard_map/hstu/pallas_call | solution.py:347
  82.2 0.8 copy.8

commit v4 on v3

--- a/solution.py
+++ b/solution.py
@@ -68,7 +68,7 @@
 def kernel(
     n, ncol, lk, win_h, wj_h, wo_h, cnt_h, usr_h, out,
     cnt, usr, tok, win, wj, wo, pay, rcv, sgp, sgr, joined, umat, okm, mixed, rpay, rrcv,
-    near2, near4, near8, wsem, lsem, xs, xr, gs, gr, fs, fr, bs, br,
+    wsem, lsem, xs, xr, gs, gr, fs, fr, bs, br,
 ):
     me = lax.axis_index("batch")
     col = lax.axis_index("col")
@@ -85,18 +85,25 @@
     def signal(sem, peer):
         pl.semaphore_signal(sem, inc=1, device_id={"batch": peer}, device_id_type=MESH)
 
-    for o in range(1, ncol):
-        pl.semaphore_signal(barrier, inc=1, device_id={"col": lax.rem(col + o, ncol)}, device_id_type=MESH)
-    signal(barrier, partner)
-    for o in (1, -1):
-        for k in (0, 1):
-            signal(barrier, 2 * at(o) + k)
-
     small = [pltpu.make_async_copy(cnt_h, cnt, lsem.at[4]), pltpu.make_async_copy(usr_h, usr, lsem.at[5])]
     for c in small:
         c.start()
     own_tok = pltpu.make_async_copy(lk.at[pl.ds(col * tokens, tokens)], tok.at[0], lsem.at[0])
     own_tok.start()
+    def greet(i, carry):
+        o = chips // 2 - i
+        for k in (0, 1):
+            signal(barrier, 2 * at(o) + k)
+            signal(barrier, 2 * at(-o) + k)
+        return carry
+
+    for k in (0, 1):
+        signal(barrier, 2 * at(chips // 2) + k)
+    lax.fori_loop(1, chips // 2, greet, 0)
+    for o in range(1, ncol):
+        pl.semaphore_signal(barrier, inc=1, device_id={"col": lax.rem(col + o, ncol)}, device_id_type=MESH)
+    signal(barrier, partner)
+
     weights = [
         pltpu.make_async_copy(
             win_h.at[pl.ds(lax.rem(col + REL[j], ncol) * slab, slab)], win.at[pl.ds(j * slab, slab)], wsem.at[0]
@@ -112,15 +119,9 @@
         peer = lax.rem(col + o, ncol)
         j = REL.index(ncol - o)
         return pltpu.make_async_remote_copy(
-            src_ref=lk.at[pl.ds(peer * tokens, tokens)], dst_ref=tok.at[j], send_sem=xs, recv_sem=xr,
+            src_ref=lk.at[pl.ds(peer * tokens, tokens)], dst_ref=tok.at[j], send_sem=xs, recv_sem=xr.at[j // 3],
             device_id={"col": peer}, device_id_type=MESH,
         )
-
-    pl.semaphore_wait(barrier, ncol - 1 + 5)
-    for o in (1, -1):
-        signal(near2, 2 * at(o) + core)
-    for o in range(1, ncol):
-        x_copy(o).start()
 
     for c in small:
         c.wait()
@@ -134,10 +135,6 @@
     start_col = jnp.sum(jnp.where(mine, starts, 0.0), axis=1, keepdims=True)
     count_col = jnp.sum(jnp.where(mine, counts, 0.0), axis=1, keepdims=True)
 
-    pl.semaphore_wait(near2, 2)
-    for o in (2, -2):
-        signal(near4, 2 * at(o) + core)
-
     lane_t = iota((rows, tokens), 1).astype(F32)
     first_r = row_r.astype(F32)
     last_r = 8.0 + (row_r & 3).astype(F32)
@@ -166,11 +163,9 @@
     def whole(buf, blocks, send, recv):
         return copy(buf.at[pl.ds(0, blocks)], buf.at[pl.ds(0, blocks)], send, recv, partner)
 
-    def send_own(peer, o):
-        copy(pay.at[peer, pl.ds(0, 1)], rcv.at[me, pl.ds(0, 1)], fs, fr.at[group_of(o)], peer).start()
-
-    def send_rest(peer, o):
-        copy(pay.at[peer, pl.ds(1, ncol - 1)], rcv.at[me, pl.ds(1, ncol - 1)], fs, fr.at[group_of(o)], peer).start()
+    def send_cols(j0, j1, peer, o):
+        cols = pl.ds(j0, j1 - j0)
+        copy(pay.at[peer, cols], rcv.at[me, cols], fs, fr.at[group_of(o)], peer).start()
 
     def send_seg(peer, o):
         copy(sgp.at[peer], sgr.at[me], gs, gr, peer).start()
@@ -185,13 +180,12 @@
                 if 2 * o != chips:
                     send(2 * at(-o) + k, o)
 
-    send_own(partner, 0)
-    send_ring(send_own, [2, 1])
-    pl.semaphore_wait(near4, 2)
-    for o in (4, -4):
-        signal(near8, 2 * at(o) + core)
-    send_ring(send_own, [4, 3])
-
+    pl.semaphore_wait(barrier, n - 1 + ncol - 1)
+    for o in (1, 3, 2):
+        x_copy(o).start()
+
+    send_cols(0, 1, partner, 0)
+    send_ring(functools.partial(send_cols, 0, 1), range(chips // 2, 0, -1))
     users = usr[...].astype(F32) + 1.0
     seg_first = jnp.sum(jnp.where(is_first, users, 0.0), axis=1, keepdims=True)
     seg_last = jnp.sum(jnp.where(is_last, users, 0.0), axis=1, keepdims=True)
@@ -202,21 +196,27 @@
     for d in range(n):
         sgp[d] = segs[d : d + 1]
 
-    pl.semaphore_wait(near8, 2)
-    send_ring(send_own, [8, 7, 6, 5])
     send_seg(partner, 0)
     send_ring(send_seg, range(chips // 2, 0, -1))
     own_seg = pltpu.make_async_copy(sgp.at[me], sgr.at[me], lsem.at[1])
     own_seg.start()
 
-    pltpu.make_async_remote_copy(
-        src_ref=tok.at[pl.ds(1, ncol - 1)], dst_ref=tok.at[pl.ds(1, ncol - 1)], send_sem=xs, recv_sem=xr,
-        device_id={"col": lax.rem(col + 1, ncol)}, device_id_type=MESH,
-    ).wait_recv()
-    for j in range(1, ncol):
-        pack(j)
-    send_rest(partner, 0)
-    send_ring(send_rest, range(chips // 2, 0, -1))
+    def x_whole(j0, j1, recv):
+        part = tok.at[pl.ds(j0, j1 - j0)]
+        return pltpu.make_async_remote_copy(
+            src_ref=part, dst_ref=part, send_sem=xs, recv_sem=recv,
+            device_id={"col": lax.rem(col + 1, ncol)}, device_id_type=MESH,
+        )
+
+    x_whole(1, 3, xr.at[0]).wait_recv()
+    pack(1)
+    pack(2)
+    send_ring(functools.partial(send_cols, 1, 3), [8, 7])
+    x_whole(3, 4, xr.at[1]).wait_recv()
+    pack(3)
+    send_ring(functools.partial(send_cols, 3, 4), [8, 7])
+    send_cols(1, 4, partner, 0)
+    send_ring(functools.partial(send_cols, 1, 4), range(chips // 2 - 2, 0, -1))
     own_pay = pltpu.make_async_copy(pay.at[me], rcv.at[me], lsem.at[2])
     own_pay.start()
 
@@ -267,12 +267,11 @@
             projected += dot(looked[j], win[j * slab : (j + 1) * slab])
         normed = layer_norm(projected.astype(BF16).astype(F32)).astype(BF16)
 
-        def project(c, carry, normed=normed, r0=r0, r1=r1):
-            cols = pl.ds(pl.multiple_of(c * WIDTH, WIDTH), WIDTH)
-            joined[r0:r1, cols] = silu(dot(normed, wj[:, cols])).astype(BF16)
-            return carry
-
-        lax.fori_loop(0, 4, project, 0)
+        def project(c0, c1, normed=normed, r0=r0, r1=r1):
+            joined[r0:r1, c0:c1] = silu(dot(normed, wj[:, c0:c1])).astype(BF16)
+
+        for c in (3, 2, 1):
+            project(c * WIDTH, (c + 1) * WIDTH)
 
         for h in range(HEADS):
             vs = slice(WIDTH + h * HEAD_DIM, WIDTH + (h + 1) * HEAD_DIM)
@@ -287,6 +286,8 @@
                 mixed[r0:r1, hs] = add[r0:] + dot((w * okm[r0:r1, 0:r0]).astype(BF16), joined[0:r0, vs])
             else:
                 mixed[0:r1, hs] = add
+            if h % 2 == 0:
+                project(h * HEAD_DIM, (h + 2) * HEAD_DIM)
 
     for a0 in range(0, chips, 2):
         gated = layer_norm(mixed[a0 * ROWS : (a0 + 2) * ROWS, :]) * joined[a0 * ROWS : (a0 + 2) * ROWS, 0:WIDTH].astype(F32)
@@ -318,10 +319,7 @@
     take_lo = (here & (lane_i < 4) & (lane_f + 8.0 == slot)).astype(F32).astype(BF16)
     take_hi = (here & (lane_i >= 4) & (lane_f + 4.0 == slot)).astype(F32).astype(BF16)
 
-    pltpu.make_async_remote_copy(
-        src_ref=tok.at[pl.ds(1, ncol - 1)], dst_ref=tok.at[pl.ds(1, ncol - 1)], send_sem=xs, recv_sem=xr,
-        device_id={"col": lax.rem(col + 1, ncol)}, device_id_type=MESH,
-    ).wait_send()
+    x_whole(1, ncol, xr.at[0]).wait_send()
     whole(sgp, n - 1, gs, gr).wait_send()
     whole(pay, n - 1, fs, fr.at[0]).wait_send()
     own_ret.wait()
@@ -367,8 +365,7 @@
             pltpu.VMEM((n * CAP, WIDTH), F32),
             pltpu.VMEM((n, 8, 3 * WIDTH // 2), BF16),
             pltpu.VMEM((n, 8, 3 * WIDTH // 2), BF16),
-            pltpu.SemaphoreType.REGULAR, pltpu.SemaphoreType.REGULAR, pltpu.SemaphoreType.REGULAR,
-            dma((3,)), dma((6,)), dma, dma, dma, dma, dma, dma((len(GROUPS),)), dma, dma,
+            dma((3,)), dma((6,)), dma, dma((2,)), dma, dma, dma, dma((len(GROUPS),)), dma, dma,
         ],
         compiler_params=pltpu.CompilerParams(collective_id=0, has_side_effects=True),
     )(lookups, input_weight, joined_weight, output_weight, owner_counts, user_index.reshape(1, tokens))

time: 83.1 us -> 80.3 us (0.966)
  Pallas kernels: 82.2 us -> 79.3 us
    pallas_call x1, Pallas kernels: 82.2 us -> 79.3 us  [on_device(): pl.pallas_call(functools.partial(kernel, n, ncol), name='hstu', out_shape...]
where the time goes in v4:
time: 80.3 us; the launch traced here: 80.1 us
  Pallas kernels  79.3 us (99%)
    pallas_call x1, Pallas kernels, on_device(): pl.pallas_call(functools.partial(kernel, n, ncol), name='hstu', out_shape...  79.3 us

profile of v4, /device:TPU:1, one launch (start us, length us, event | category | flops | bytes accessed | tf_op | source)
XLA Modules:
  0.0 80.1 jit_solution(4483264807646892002)
XLA Ops:
  0.0 79.3 %hstu.1 = bf16[256,1024]{1,0:T(8,128)(2,1)S(1)} custom-call(bf16[1024,256]{1,0:T(8,128)(2,1)} %lk.1, bf16[1024,1024]{1,0:T(8,128)(2,1)} %win_h.1, bf16[1024,2048]{1,0:T(8,128)(2,1)} %wj_h.1, bf16[512,1024]{1,0:T(8,128)(2,1)} %wo_h.1, s32[1,32]{1,0:T(1,128)} %cnt_h.1, s32[1,256]{1,0:T(1,128)} %bitcast.1), custom_call_target="tpu_custom_call" | custom-call | tf_op jit(solution)/shard_map/hstu/pallas_call | solution.py:345
  79.4 0.8 copy.8

commit v5 on v4

--- a/solution.py
+++ b/solution.py
@@ -224,7 +224,7 @@
     hidden = dot(tok[0], win[0:slab])
     for j in range(1, ncol):
         hidden += dot(tok[j], win[j * slab : (j + 1) * slab])
-    hidden = hidden.astype(BF16)
+    out[...] = hidden.astype(BF16)
 
     low = iota((1, 8, 1), 1) < 4
     low8 = iota((8, 1), 0) < 4
@@ -250,6 +250,24 @@
 
     weights[ncol].wait()
     own_pay.wait()
+    def give_back(b0, b1):
+        for a0 in range(b0, b1, 2):
+            part = slice(a0 * ROWS, (a0 + 2) * ROWS)
+            gated = layer_norm(mixed[part, :]) * joined[part, 0:WIDTH].astype(F32)
+            for a in (a0 + 1, a0):
+                zz = at(OFFSETS[a])
+                g = gated[(a - a0) * ROWS : (a - a0 + 1) * ROWS]
+                e_lo, e_hi = g[16:24, : WIDTH // 2], g[16:24, WIDTH // 2 :]
+                rpay[2 * zz, :, 0:WIDTH] = g[0:8].astype(BF16)
+                rpay[2 * zz, :, WIDTH:] = jnp.where(low8, e_lo, pltpu.roll(e_hi, 4, 0)).astype(BF16)
+                rpay[2 * zz + 1, :, 0:WIDTH] = g[8:16].astype(BF16)
+                rpay[2 * zz + 1, :, WIDTH:] = jnp.where(low8, pltpu.roll(e_lo, 4, 0), e_hi).astype(BF16)
+                if a == 0:
+                    send_back(partner, 0)
+                else:
+                    for k in (0, 1):
+                        send_back(2 * zz + k, OFFSETS[a])
+
     for g, (a0, a1) in enumerate(GROUPS):
         whole(rcv, 2 * (a1 - a0) - (a0 == 0), fs, fr.at[g]).wait_recv()
         parts = []
@@ -270,40 +288,36 @@
         def project(c0, c1, normed=normed, r0=r0, r1=r1):
             joined[r0:r1, c0:c1] = silu(dot(normed, wj[:, c0:c1])).astype(BF16)
 
-        for c in (3, 2, 1):
-            project(c * WIDTH, (c + 1) * WIDTH)
-
+        def add_new(q0, q1, h):
+            hs = slice(h * HEAD_DIM, (h + 1) * HEAD_DIM)
+            vs, qs, ks = (slice(c * WIDTH + hs.start, c * WIDTH + hs.stop) for c in (1, 2, 3))
+            w = silu(dot_nt(joined[q0:q1, qs], joined[r0:r1, ks]), HEAD_DIM ** (-0.5))
+            add = dot((w * okm[q0:q1, r0:r1]).astype(BF16), joined[r0:r1, vs])
+            old = min(q1, r0)
+            if old > q0:
+                mixed[q0:old, hs] += add[: old - q0]
+            if q1 > r0:
+                if r0:
+                    w = silu(dot_nt(joined[r0:r1, qs], joined[0:r0, ks]), HEAD_DIM ** (-0.5))
+                    mixed[r0:r1, hs] = add[r0 - q0 :] + dot((w * okm[r0:r1, 0:r0]).astype(BF16), joined[0:r0, vs])
+                else:
+                    mixed[0:r1, hs] = add
+
+        project(3 * WIDTH, 4 * WIDTH)
+        project(WIDTH, 2 * WIDTH)
+        q0 = 0
+        if a1 == chips:
+            q0 = GROUPS[0][1] * ROWS
+            for h in range(HEADS):
+                add_new(0, q0, h)
+            give_back(0, GROUPS[0][1])
+        project(2 * WIDTH, 3 * WIDTH)
         for h in range(HEADS):
-            vs = slice(WIDTH + h * HEAD_DIM, WIDTH + (h + 1) * HEAD_DIM)
-            qs = slice(2 * WIDTH + h * HEAD_DIM, 2 * WIDTH + (h + 1) * HEAD_DIM)
-            ks = slice(3 * WIDTH + h * HEAD_DIM, 3 * WIDTH + (h + 1) * HEAD_DIM)
-            hs = slice(h * HEAD_DIM, (h + 1) * HEAD_DIM)
-            w = silu(dot_nt(joined[0:r1, qs], joined[r0:r1, ks]), HEAD_DIM ** (-0.5))
-            add = dot((w * okm[0:r1, r0:r1]).astype(BF16), joined[r0:r1, vs])
-            if r0:
-                mixed[0:r0, hs] += add[:r0]
-                w = silu(dot_nt(joined[r0:r1, qs], joined[0:r0, ks]), HEAD_DIM ** (-0.5))
-                mixed[r0:r1, hs] = add[r0:] + dot((w * okm[r0:r1, 0:r0]).astype(BF16), joined[0:r0, vs])
-            else:
-                mixed[0:r1, hs] = add
+            add_new(q0, r1, h)
             if h % 2 == 0:
                 project(h * HEAD_DIM, (h + 2) * HEAD_DIM)
 
-    for a0 in range(0, chips, 2):
-        gated = layer_norm(mixed[a0 * ROWS : (a0 + 2) * ROWS, :]) * joined[a0 * ROWS : (a0 + 2) * ROWS, 0:WIDTH].astype(F32)
-        for a in (a0 + 1, a0):
-            zz = at(OFFSETS[a])
-            g = gated[(a - a0) * ROWS : (a - a0 + 1) * ROWS]
-            e_lo, e_hi = g[16:24, : WIDTH // 2], g[16:24, WIDTH // 2 :]
-            rpay[2 * zz, :, 0:WIDTH] = g[0:8].astype(BF16)
-            rpay[2 * zz, :, WIDTH:] = jnp.where(low8, e_lo, pltpu.roll(e_hi, 4, 0)).astype(BF16)
-            rpay[2 * zz + 1, :, 0:WIDTH] = g[8:16].astype(BF16)
-            rpay[2 * zz + 1, :, WIDTH:] = jnp.where(low8, pltpu.roll(e_lo, 4, 0), e_hi).astype(BF16)
-            if a == 0:
-                send_back(partner, 0)
-            else:
-                for k in (0, 1):
-                    send_back(2 * zz + k, OFFSETS[a])
+    give_back(GROUPS[0][1], chips)
     own_ret = pltpu.make_async_copy(rpay.at[me], rrcv.at[me], lsem.at[3])
     own_ret.start()
 
@@ -332,7 +346,7 @@
     gated_lo = gated[:, : WIDTH // 2] + dot(take_lo, back_x)
     gated_hi = gated[:, WIDTH // 2 :] + dot(take_hi, back_x)
     branch = dot(gated_lo.astype(BF16), wo[: WIDTH // 2]) + dot(gated_hi.astype(BF16), wo[WIDTH // 2 :])
-    out[...] = (hidden.astype(F32) + branch.astype(BF16).astype(F32)).astype(BF16)
+    out[...] = (out[...].astype(F32) + branch.astype(BF16).astype(F32)).astype(BF16)
 
     whole(rpay, n - 1, bs, br).wait_send()
 

time: 80.3 us -> 79.1 us (0.985)
  Pallas kernels: 79.3 us -> 78.1 us
    pallas_call x1, Pallas kernels: 79.3 us -> 78.1 us  [on_device(): pl.pallas_call(functools.partial(kernel, n, ncol), name='hstu', out_shape...]
where the time goes in v5:
time: 79.1 us; the launch traced here: 79 us
  Pallas kernels  78.1 us (99%)
  local copies, waits for them, and re-layouts  0.8 us (1%)
    pallas_call x1, Pallas kernels, on_device(): pl.pallas_call(functools.partial(kernel, n, ncol), name='hstu', out_shape...  78.1 us

profile of v5, /device:TPU:1, one launch (start us, length us, event | category | flops | bytes accessed | tf_op | source)
XLA Modules:
  0.0 79.0 jit_solution(10527654671154512601)
XLA Ops:
  0.0 78.1 %hstu.1 = bf16[256,1024]{1,0:T(8,128)(2,1)S(1)} custom-call(bf16[1024,256]{1,0:T(8,128)(2,1)} %lk.1, bf16[1024,1024]{1,0:T(8,128)(2,1)} %win_h.1, bf16[1024,2048]{1,0:T(8,128)(2,1)} %wj_h.1, bf16[512,1024]{1,0:T(8,128)(2,1)} %wo_h.1, s32[1,32]{1,0:T(1,128)} %cnt_h.1, s32[1,256]{1,0:T(1,128)} %bitcast.1), custom_call_target="tpu_custom_call" | custom-call | tf_op jit(solution)/shard_map/hstu/pallas_call | solution.py:359
  78.2 0.8 %copy.8 = bf16[256,1024]{1,0:T(8,128)(2,1)} copy(bf16[256,1024]{1,0:T(8,128)(2,1)S(1)} %hstu.1) | data formatting | bytes 1048576

commit v6 on v5

--- a/solution.py
+++ b/solution.py
@@ -268,6 +268,15 @@
                     for k in (0, 1):
                         send_back(2 * zz + k, OFFSETS[a])
 
+    far = GROUPS[0][1] * ROWS
+
+    def attend(q0, q1, k0, k1, h, add):
+        hs = slice(h * HEAD_DIM, (h + 1) * HEAD_DIM)
+        vs, qs, ks = (slice(c * WIDTH + hs.start, c * WIDTH + hs.stop) for c in (1, 2, 3))
+        w = silu(dot_nt(joined[q0:q1, qs], joined[k0:k1, ks]), HEAD_DIM ** (-0.5))
+        new = dot((w * okm[q0:q1, k0:k1]).astype(BF16), joined[k0:k1, vs])
+        mixed[q0:q1, hs] = mixed[q0:q1, hs] + new if add else new
+
     for g, (a0, a1) in enumerate(GROUPS):
         whole(rcv, 2 * (a1 - a0) - (a0 == 0), fs, fr.at[g]).wait_recv()
         parts = []
@@ -288,35 +297,25 @@
         def project(c0, c1, normed=normed, r0=r0, r1=r1):
             joined[r0:r1, c0:c1] = silu(dot(normed, wj[:, c0:c1])).astype(BF16)
 
-        def add_new(q0, q1, h):
-            hs = slice(h * HEAD_DIM, (h + 1) * HEAD_DIM)
-            vs, qs, ks = (slice(c * WIDTH + hs.start, c * WIDTH + hs.stop) for c in (1, 2, 3))
-            w = silu(dot_nt(joined[q0:q1, qs], joined[r0:r1, ks]), HEAD_DIM ** (-0.5))
-            add = dot((w * okm[q0:q1, r0:r1]).astype(BF16), joined[r0:r1, vs])
-            old = min(q1, r0)
-            if old > q0:
-                mixed[q0:old, hs] += add[: old - q0]
-            if q1 > r0:
-                if r0:
-                    w = silu(dot_nt(joined[r0:r1, qs], joined[0:r0, ks]), HEAD_DIM ** (-0.5))
-                    mixed[r0:r1, hs] = add[r0 - q0 :] + dot((w * okm[r0:r1, 0:r0]).astype(BF16), joined[0:r0, vs])
-                else:
-                    mixed[0:r1, hs] = add
-
         project(3 * WIDTH, 4 * WIDTH)
         project(WIDTH, 2 * WIDTH)
-        q0 = 0
+        if a0 == 0:
+            project(2 * WIDTH, 3 * WIDTH)
+        for h in range(HEADS):
+            attend(0, far, r0, r1, h, g > 0)
+            if a0 == 0 and h % 2 == 0:
+                project(h * HEAD_DIM, (h + 2) * HEAD_DIM)
         if a1 == chips:
-            q0 = GROUPS[0][1] * ROWS
-            for h in range(HEADS):
-                add_new(0, q0, h)
             give_back(0, GROUPS[0][1])
-        project(2 * WIDTH, 3 * WIDTH)
-        for h in range(HEADS):
-            add_new(q0, r1, h)
-            if h % 2 == 0:
-                project(h * HEAD_DIM, (h + 2) * HEAD_DIM)
-
+        if a0:
+            project(2 * WIDTH, 3 * WIDTH)
+            if a1 < chips:
+                project(0, WIDTH)
+
+    for h in range(HEADS):
+        attend(far, n * CAP, 0, n * CAP, h, False)
+        if h % 2 == 0:
+            project(h * HEAD_DIM, (h + 2) * HEAD_DIM)
     give_back(GROUPS[0][1], chips)
     own_ret = pltpu.make_async_copy(rpay.at[me], rrcv.at[me], lsem.at[3])
     own_ret.start()

time: 79.1 us -> 79.3 us (level)
  no operation moved by 1% of the time
where the time goes in v6:
time: 79.3 us; the launch traced here: 79.2 us
  Pallas kernels  78.4 us (99%)
  local copies, waits for them, and re-layouts  0.8 us (1%)
    pallas_call x1, Pallas kernels, on_device(): pl.pallas_call(functools.partial(kernel, n, ncol), name='hstu', out_shape...  78.4 us

profile of v6, /device:TPU:1, one launch (start us, length us, event | category | flops | bytes accessed | tf_op | source)
XLA Modules:
  0.0 79.2 jit_solution(3962876991078057548)
XLA Ops:
  0.0 78.4 %hstu.1 = bf16[256,1024]{1,0:T(8,128)(2,1)S(1)} custom-call(bf16[1024,256]{1,0:T(8,128)(2,1)} %lk.1, bf16[1024,1024]{1,0:T(8,128)(2,1)} %win_h.1, bf16[1024,2048]{1,0:T(8,128)(2,1)} %wj_h.1, bf16[512,1024]{1,0:T(8,128)(2,1)} %wo_h.1, s32[1,32]{1,0:T(1,128)} %cnt_h.1, s32[1,256]{1,0:T(1,128)} %bitcast.1), custom_call_target="tpu_custom_call" | custom-call | tf_op jit(solution)/shard_map/hstu/pallas_call | solution.py:358
  78.4 0.8 %copy.8 = bf16[256,1024]{1,0:T(8,128)(2,1)} copy(bf16[256,1024]{1,0:T(8,128)(2,1)S(1)} %hstu.1) | data formatting | bytes 1048576
